TPU v7x, 512 devices: a whole 4x8x8 slice. The times are simulated.
512 devices in a mesh: member: 4 (over y_lo), space: 128 (over x, y_hi, z, core).
Axes of the slice: x: 4, y: 8 (y_hi: 2, y_lo: 4; y = y_hi * 4 + y_lo), z: 8, core: 2. Of those that a mesh axis runs over, the one named last changes fastest.
Arguments:
- initial_fields: bfloat16 [128, 64, 16384], P('member', None, 'space'), may hold values from -4 to 4
- encode_weight: bfloat16 [64, 256], replicated, may hold values from -0.75 to 0.75
- send_weight: bfloat16 [1, 256, 256], replicated, may hold values from -0.375 to 0.375
- receive_weight: bfloat16 [1, 256, 256], replicated, may hold values from -0.375 to 0.375
- update_weight: bfloat16 [1, 256, 256], replicated, may hold values from -0.375 to 0.375
- norm_gain: bfloat16 [1, 256], replicated, may hold values from 0.099609375 to 1.8984375
- decode_weight: bfloat16 [256, 64], replicated, may hold values from -0.375 to 0.375
- edge_senders: int32 [16384, 4], P('space'), may hold values from 0 to 191
- halo_nodes: int32 [2, 4096], P(None, 'space'), may hold values from 0 to 127, as said below
- observed_perturbation: bfloat16 [512, 128, 256], P(('member', 'space')), may hold values from -2.5 to 2.5
- observed_values: bfloat16 [512, 2, 256], P(('member', 'space')), may hold values from -3.5 to 3.5, as said below
- region_neighbours: int32 [512, 8], P(('member', 'space')), may hold values from 0 to 511, as said below
Outputs:
- analysis: bfloat16 [128, 64, 16384], P('member', None, 'space')
Inputs may be any that keep to these rules, and one draw needn't show every extreme that they name: edge_senders[n, k] indexes the list of the 128 nodes of n's space block, followed by the 32 nodes that halo_nodes row 0 names in the block before and the 32 that row 1 names in the block after (blocks wrap around). For each space block b, halo_nodes[0, b * 32 : (b + 1) * 32] are distinct node indices within block b - 1 and halo_nodes[1, ...] distinct ones within block b + 1, taken modulo 128. `region_neighbours`: each row lists 8 distinct regions other than r = a * 128 + b; each is ((a + p) mod 4) * 128 + ((b + s) mod 128) with either p = 0 and 1 <= |s| <= 2, or |p| = 1 and |s| <= 1. `observed_values`: row 0 of each region holds positive inverse error variances of at least 0.25.
All inputs are finite; a program needn't handle non-finite values.
Results may differ from a plain program's by a relative error of at most 0.0059.
Values may be sent and summed in bfloat16 or wider, within the bound.
A program may use at most 64 MiB of HBM per device.

v0:
```python
import jax
import jax.numpy as jnp
from jax import lax
from jax.sharding import PartitionSpec as P

ITERS_NS = 5


EPSILON = 1e-05
FULL_PRECISION = lax.Precision.HIGHEST


def extended_2(cells, sides, width):
    for axis, dim in sides:
        count = lax.axis_size(axis)
        head = lax.slice_in_dim(cells, 0, width, axis=dim)
        tail = lax.slice_in_dim(cells, cells.shape[dim] - width, cells.shape[dim], axis=dim)
        cells = jnp.concatenate(
            [
                lax.ppermute(tail, axis, [(i, (i + 1) % count) for i in range(count)]),
                cells,
                lax.ppermute(head, axis, [((i + 1) % count, i) for i in range(count)]),
            ],
            axis=dim,
        )
    return cells


def normalize(messages, gains):
    mean_square = jnp.mean(messages * messages, axis=-1, keepdims=True)
    return messages * lax.rsqrt(mean_square + EPSILON) * gains.astype(jnp.float32)


def inverse_root(system):
    extent = system.shape[0]
    identity = jnp.eye(extent, dtype=jnp.float32)
    scaling = jnp.sqrt(jnp.sum(system * system))
    iterate = system / scaling
    inverse = identity
    for _ in range(ITERS_NS):
        correction = 1.5 * identity - 0.5 * jnp.dot(inverse, iterate, precision=FULL_PRECISION)
        iterate = jnp.dot(iterate, correction, precision=FULL_PRECISION)
        inverse = jnp.dot(correction, inverse, precision=FULL_PRECISION)
    return (inverse, scaling)


def analyse(states, gram_matrix, forcing):
    ensemble = states.shape[0]
    identity = jnp.eye(ensemble, dtype=jnp.float32)
    system = identity + gram_matrix / (ensemble - 1)
    inverse, scaling = inverse_root(system)
    inner = jnp.dot(inverse, forcing, precision=FULL_PRECISION)
    mean_weights = jnp.dot(inverse, inner, precision=FULL_PRECISION) / (scaling * (ensemble - 1))
    transform = inverse / jnp.sqrt(scaling) + mean_weights[:, None]
    mean_state = jnp.mean(states, axis=0)
    anomalies = states - mean_state
    moved = jnp.einsum("ij,is->js", transform, anomalies, precision=FULL_PRECISION)
    return (mean_state + moved).astype(jnp.bfloat16)


def offsets(neighbours, own_row, own_column, row_count, column_count):
    near_row = (neighbours // column_count - own_row + 1) % row_count - 1
    near_column = (neighbours % column_count - own_column + 2) % column_count - 2
    distance = (near_row * near_row + near_column * near_column).astype(jnp.float32)
    return (near_row, near_column, 1.0 / (1.0 + distance / 2.0))


def collect(square, framed):
    flat = square.reshape((9,) + square.shape[2:])
    return jnp.concatenate([flat, framed[0:1], framed[3:4]], axis=0)


def body(
    initial_fields,
    encode_weight,
    send_weight,
    receive_weight,
    update_weight,
    norm_gain,
    decode_weight,
    edge_senders,
    halo_nodes,
    observed_perturbation,
    observed_values,
    region_neighbours,
):
    halo_count = halo_nodes.shape[1]
    stream = jnp.einsum(
        "mcn,ch->mnh", initial_fields, encode_weight, preferred_element_type=jnp.float32
    )
    wanted = extended_2(halo_nodes, (("space", 1),), halo_count)
    picked = jnp.concatenate([wanted[1, :halo_count], wanted[0, 2 * halo_count :]])
    rounded = stream.astype(jnp.bfloat16)
    sent = jnp.einsum(
        "mnh,hk->mnk", rounded, send_weight[0], preferred_element_type=jnp.float32
    ).astype(jnp.bfloat16)
    received = jnp.einsum(
        "mnh,hk->mnk", rounded, receive_weight[0], preferred_element_type=jnp.float32
    )
    outgoing = jnp.take(sent, picked, axis=1)
    framed_rows = extended_2(outgoing, (("space", 1),), halo_count)
    extended = jnp.concatenate(
        [sent, framed_rows[:, :halo_count], framed_rows[:, 3 * halo_count :]], axis=1
    )
    messages = jnp.zeros_like(received)
    for slot_index in range(edge_senders.shape[1]):
        sender_rows = jnp.take(extended, edge_senders[:, slot_index], axis=1)
        messages = messages + jax.nn.silu(sender_rows.astype(jnp.float32) + received)
    normed = normalize(messages, norm_gain[0]).astype(jnp.bfloat16)
    stream = stream + jnp.einsum(
        "mnh,hk->mnk", normed, update_weight[0], preferred_element_type=jnp.float32
    )
    field_change = jnp.einsum(
        "mnh,hc->mcn",
        stream.astype(jnp.bfloat16),
        decode_weight,
        preferred_element_type=jnp.float32,
    )
    predicted_fields = (initial_fields.astype(jnp.float32) + field_change).astype(jnp.bfloat16)
    regional_states = lax.all_to_all(
        predicted_fields, "member", split_axis=2, concat_axis=0, tiled=True
    )
    ensemble = regional_states.shape[0]
    states = regional_states.reshape(ensemble, -1).astype(jnp.float32)
    near_row, near_column, weights = offsets(
        region_neighbours[0],
        lax.axis_index("member"),
        lax.axis_index("space"),
        lax.axis_size("member"),
        lax.axis_size("space"),
    )
    slot = jnp.where(
        near_column == -2, 9, jnp.where(near_column == 2, 10, (near_row + 1) * 3 + near_column + 1)
    )
    slot_range = jnp.arange(11, dtype=jnp.int32)
    slot_weight = jnp.sum(
        weights[:, None] * (slot[:, None] == slot_range[None, :]).astype(jnp.float32), axis=0
    )
    slot_weight = slot_weight + (slot_range == 4).astype(jnp.float32)
    perturbation = observed_perturbation[0]
    values = observed_values[0].astype(jnp.float32)
    wide_perturbation = perturbation.astype(jnp.float32)
    local_gram = jnp.einsum(
        "io,jo->ij",
        wide_perturbation * values[0][None, :],
        wide_perturbation,
        precision=FULL_PRECISION,
    )
    local_forcing = jnp.dot(wide_perturbation, values[0] * values[1], precision=FULL_PRECISION)
    payload = jnp.concatenate([local_gram, local_forcing[None, :]], axis=0)[None, None]
    square = extended_2(payload, (("member", 0), ("space", 1)), 1)
    paired = jnp.stack([square[1, 2], square[1, 0]])
    framed = extended_2(paired.astype(jnp.bfloat16), (("space", 0),), 1).astype(paired.dtype)
    candidates = collect(square, framed)
    gram_matrix = jnp.einsum(
        "c,cij->ij", slot_weight, candidates[:, :ensemble], precision=FULL_PRECISION
    )
    forcing = jnp.dot(slot_weight, candidates[:, ensemble], precision=FULL_PRECISION)
    analysed = analyse(states, gram_matrix, forcing).reshape(regional_states.shape)
    return lax.all_to_all(analysed, "member", split_axis=0, concat_axis=2, tiled=True)


def solution(mesh):
    placed = (
        P("member", None, "space"),
        P(),
        P(),
        P(),
        P(),
        P(),
        P(),
        P("space", None),
        P(None, "space"),
        P(("member", "space"), None, None),
        P(("member", "space"), None, None),
        P(("member", "space"), None),
    )
    return jax.shard_map(
        body, mesh=mesh, in_specs=placed, out_specs=P("member", None, "space"), check_vma=False
    )
```

profile of v0, /device:TPU:8, one launch (start us, length us, event | category | flops | bytes accessed | tf_op | source)
XLA Modules:
  0.0 173.3 jit_solution(415992370477055487)
XLA Ops:
  0.0 17.1 %collective-permute-start.1 = (s32[2,32]{1,0:T(2,128)}, s32[2,32]{1,0:T(2,128)S(1)}, u32[]{:S(2)}, u32[]{:S(2)}) collective-permute-start(s32[2,32]{1,0:T(2,128)} %param.22), channel_id=1, source_target_pairs={{1,0},{2,1},{3,2},{4,3},{5,4},{6,5},{7,6},{8,7},{9,8},{10,9},{11,1... | collective-permute-start | bytes 776 | tf_op jit(solution)/shard_map/ppermute | solution.py:22
  17.1 1.9 %collective-permute-start = (s32[2,32]{1,0:T(2,128)}, s32[2,32]{1,0:T(2,128)S(1)}, u32[]{:S(2)}, u32[]{:S(2)}) collective-permute-start(s32[2,32]{1,0:T(2,128)} %param.22), channel_id=1, source_target_pairs={{0,1},{1,2},{2,3},{3,4},{4,5},{5,6},{6,7},{7,8},{8,9},{9,10},{10,1... | collective-permute-start | bytes 776 | tf_op jit(solution)/shard_map/ppermute | solution.py:20
  21.3 1.2 fusion.20
  22.6 3.3 %collective-permute-start.5 = (f32[1,1,129,128]{3,2,1,0:T(8,128)S(1)}, f32[1,1,129,128]{3,2,1,0:T(8,128)S(1)}, u32[]{:S(2)}, u32[]{:S(2)}) collective-permute-start(f32[1,1,129,128]{3,2,1,0:T(8,128)S(1)} %maximum_bitcast_fusion), channel_id=1, source_target_pairs={{128,0},{256,128},{384,256},{0,384},{129,1},{257,129},{385,257},{1... | collective-permute-start | bytes 198152 | tf_op jit(solution)/shard_map/ppermute | solution.py:22
  25.8 2.6 %collective-permute-start.4 = (f32[1,1,129,128]{3,2,1,0:T(8,128)S(1)}, f32[1,1,129,128]{3,2,1,0:T(8,128)S(1)}, u32[]{:S(2)}, u32[]{:S(2)}) collective-permute-start(f32[1,1,129,128]{3,2,1,0:T(8,128)S(1)} %maximum_bitcast_fusion), channel_id=1, source_target_pairs={{0,128},{128,256},{256,384},{384,0},{1,129},{129,257},{257,385},{3... | collective-permute-start | bytes 198152 | tf_op jit(solution)/shard_map/ppermute | solution.py:20
  29.3 1.8 %fusion.40 = f32[32,128,256]{2,1,0:T(8,128)S(1)} fusion(bf16[32,64,128]{2,1,0:T(8,128)(2,1)} %param.14, bf16[64,256]{1,0:T(8,128)(2,1)} %param.15), kind=kOutput, calls=%fused_computation.78 | convolution fusion | flops 134217728 | bytes 4751360 | tf_op jit(solution)/shard_map/mcn,ch->mnh/dot_general | solution.py:88
  32.0 2.5 %copy.107 = bf16[32,128,256]{2,0,1:T(8,128)(2,1)} copy(bf16[32,128,256]{2,1,0:T(8,128)(2,1)S(1)} %convolution_convert_fusion) | data formatting | bytes 4194304 | tf_op jit(solution)/shard_map/convert_element_type | solution.py:96
  34.6 2.2 %gather_fusion = bf16[64,32,256]{2,1,0:T(8,128)(2,1)S(1)} fusion(bf16[32,128,256]{2,0,1:T(8,128)(2,1)} %copy.107, s32[1024]{0:T(1024)S(1)} %pad_clamp_fusion.4), kind=kCustom, calls=%fused_computation.4 | custom fusion | bytes 2097408 | tf_op jit(solution)/shard_map/jit(_take)/gather | solution.py:100
  37.6 11.2 %collective-permute-start.7 = (f32[3,1,129,128]{3,2,1,0:T(8,128)S(1)}, f32[3,1,129,128]{3,2,1,0:T(8,128)S(1)}, u32[]{:S(2)}, u32[]{:S(2)}) collective-permute-start(f32[3,1,129,128]{3,2,1,0:T(8,128)S(1)} %pad_maximum_fusion.3), channel_id=1, source_target_pairs={{1,0},{2,1},{3,2},{4,3},{5,4},{6,5},{7,6},{8,7},{9,8},{10,9},{11,1... | collective-permute-start | bytes 594440 | tf_op jit(solution)/shard_map/ppermute | solution.py:22
  49.9 1.9 %collective-permute-start.3 = (bf16[32,32,256]{2,1,0:T(8,128)(2,1)}, bf16[32,32,256]{2,1,0:T(8,128)(2,1)}, u32[]{:S(2)}, u32[]{:S(2)}) collective-permute-start(bf16[32,32,256]{2,1,0:T(8,128)(2,1)} %get-tuple-element.18), channel_id=1, source_target_pairs={{1,0},{2,1},{3,2},{4,3},{5,4},{6,5},{7,6},{8,7},{9,8},{10,9},{11,1... | collective-permute-start | bytes 1572872 | tf_op jit(solution)/shard_map/ppermute | solution.py:22
  51.8 2.4 %collective-permute-start.2 = (bf16[32,32,256]{2,1,0:T(8,128)(2,1)}, bf16[32,32,256]{2,1,0:T(8,128)(2,1)}, u32[]{:S(2)}, u32[]{:S(2)}) collective-permute-start(bf16[32,32,256]{2,1,0:T(8,128)(2,1)} %get-tuple-element.17), channel_id=1, source_target_pairs={{0,1},{1,2},{2,3},{3,4},{4,5},{5,6},{6,7},{7,8},{8,9},{9,10},{10,1... | collective-permute-start | bytes 1572872 | tf_op jit(solution)/shard_map/ppermute | solution.py:20
  54.2 1.9 %collective-permute-start.6 = (f32[3,1,129,128]{3,2,1,0:T(8,128)S(1)}, f32[3,1,129,128]{3,2,1,0:T(8,128)S(1)}, u32[]{:S(2)}, u32[]{:S(2)}) collective-permute-start(f32[3,1,129,128]{3,2,1,0:T(8,128)S(1)} %pad_maximum_fusion.3), channel_id=1, source_target_pairs={{0,1},{1,2},{2,3},{3,4},{4,5},{5,6},{6,7},{7,8},{8,9},{9,10},{10,1... | collective-permute-start | bytes 594440 | tf_op jit(solution)/shard_map/ppermute | solution.py:20
  56.2 11.8 %collective-permute-start.9 = (bf16[1,129,128]{2,1,0:T(8,128)(2,1)S(1)}, bf16[1,129,128]{2,1,0:T(8,128)(2,1)S(1)}, u32[]{:S(2)}, u32[]{:S(2)}) collective-permute-start(bf16[1,129,128]{2,1,0:T(8,128)(2,1)S(1)} %fusion.37), channel_id=1, source_target_pairs={{1,0},{2,1},{3,2},{4,3},{5,4},{6,5},{7,6},{8,7},{9,8},{10,9},{11,1... | collective-permute-start | bytes 99080 | tf_op jit(solution)/shard_map/ppermute | solution.py:22
  68.0 12.8 %collective-permute-done.6 = f32[3,1,129,128]{3,2,1,0:T(8,128)S(1)} collective-permute-done((f32[3,1,129,128]{3,2,1,0:T(8,128)S(1)}, f32[3,1,129,128]{3,2,1,0:T(8,128)S(1)}, u32[]{:S(2)}, u32[]{:S(2)}) %collective-permute-start.6) | collective-permute-done | bytes 198176 | tf_op jit(solution)/shard_map/ppermute | solution.py:20
  80.8 1.9 %collective-permute-start.8 = (bf16[1,129,128]{2,1,0:T(8,128)(2,1)S(1)}, bf16[1,129,128]{2,1,0:T(8,128)(2,1)S(1)}, u32[]{:S(2)}, u32[]{:S(2)}) collective-permute-start(bf16[1,129,128]{2,1,0:T(8,128)(2,1)S(1)} %fusion.36), channel_id=1, source_target_pairs={{0,1},{1,2},{2,3},{3,4},{4,5},{5,6},{6,7},{7,8},{8,9},{9,10},{10,1... | collective-permute-start | bytes 99080 | tf_op jit(solution)/shard_map/ppermute | solution.py:20
  82.7 11.4 %collective-permute-done.8 = bf16[1,129,128]{2,1,0:T(8,128)(2,1)S(1)} collective-permute-done((bf16[1,129,128]{2,1,0:T(8,128)(2,1)S(1)}, bf16[1,129,128]{2,1,0:T(8,128)(2,1)S(1)}, u32[]{:S(2)}, u32[]{:S(2)}) %collective-permute-start.8) | collective-permute-done | bytes 33056 | tf_op jit(solution)/shard_map/ppermute | solution.py:20
  99.4 2.3 %pad_maximum_fusion = bf16[32,192,256]{2,1,0:T(8,128)(2,1)S(1)} fusion(bf16[32,32,256]{2,1,0:T(8,128)(2,1)} %collective-permute-done.3, bf16[32,32,256]{2,1,0:T(8,128)(2,1)} %collective-permute-done.2, bf16[32,128,256]{2,1,0:T(8,128)(2,1)S(1)} %convolution_convert_fusion), kind=kLoop, calls=%fused_computation.9 | loop fusion | flops 9437184 | bytes 6291456 | tf_op jit(solution)/shard_map/concatenate | solution.py:102
  101.6 1.8 %copy.109 = bf16[32,192,256]{2,0,1:T(8,128)(2,1)S(1)} copy(bf16[32,192,256]{2,1,0:T(8,128)(2,1)S(1)} %pad_maximum_fusion) | data formatting | bytes 6291456 | tf_op jit(solution)/shard_map/concatenate | solution.py:102
  103.4 2.1 %gather_fusion.4 = bf16[128,32,256]{2,1,0:T(8,128)(2,1)} fusion(bf16[32,192,256]{2,0,1:T(8,128)(2,1)S(1)} %copy.109, s32[1024]{0:T(1024)S(1)} %get-tuple-element.33), kind=kCustom, calls=%fused_computation.3.clone | custom fusion | bytes 4194816 | tf_op jit(solution)/shard_map/jit(_take)/gather | solution.py:107
  105.5 2.0 %gather_fusion.3 = bf16[128,32,256]{2,1,0:T(8,128)(2,1)} fusion(bf16[32,192,256]{2,0,1:T(8,128)(2,1)S(1)} %copy.109, s32[1024]{0:T(1024)S(1)} %get-tuple-element.34), kind=kCustom, calls=%fused_computation.2.clone | custom fusion | bytes 4194816 | tf_op jit(solution)/shard_map/jit(_take)/gather | solution.py:107
  107.5 2.0 %gather_fusion.2 = bf16[128,32,256]{2,1,0:T(8,128)(2,1)} fusion(bf16[32,192,256]{2,0,1:T(8,128)(2,1)S(1)} %copy.109, s32[1024]{0:T(1024)S(1)} %get-tuple-element.35), kind=kCustom, calls=%fused_computation.1.clone | custom fusion | bytes 4194816 | tf_op jit(solution)/shard_map/jit(_take)/gather | solution.py:107
  109.5 2.0 %gather_fusion.1 = bf16[128,32,256]{2,1,0:T(8,128)(2,1)} fusion(bf16[32,192,256]{2,0,1:T(8,128)(2,1)S(1)} %copy.109, s32[1024]{0:T(1024)S(1)} %get-tuple-element.36), kind=kCustom, calls=%fused_computation.clone | custom fusion | bytes 4194816 | tf_op jit(solution)/shard_map/jit(_take)/gather | solution.py:107
  111.5 13.8 %multiply_reduce_fusion = (f32[32,128]{1,0:T(8,128)S(1)}, f32[32,128,256]{2,1,0:T(8,128)}) fusion(bf16[128,32,256]{2,1,0:T(8,128)(2,1)} %gather_fusion.4, pred[128]{0:T(512)(128)(4,1)S(1)} %get-tuple-element.23, bf16[128,32,256]{2,1,0:T(8,128)(2,1)} %gather_fusion.3, pred[128]{0:T(512)(128)(4,1)S(1)} %get-tuple-element.25, ...), kind=kOutput, calls=%fused_computation.7 | convolution fusion | flops 572518400 | bytes 16925184 | tf_op jit(solution)/shard_map/mnh,hk->mnk/dot_general | solution.py:97
  125.3 4.9 %fusion.6 = bf16[32,64,128]{2,1,0:T(8,128)(2,1)S(1)} fusion(f32[32,128,256]{2,1,0:T(8,128)} %copy-done.1, f32[32,128,256]{2,1,0:T(8,128)} %get-tuple-element.32, f32[256]{0:T(256)S(1)} %bitcast.179, f32[32,128]{1,0:T(8,128)S(1)} %add_rsqrt_fusion, bf16[32,64,128]{2,1,0:T(8,128)(2,1)S(1)} %copy-done.2, bf16[1,256,256]{2,1,0:T(8,128)(2,1)S(1)} %copy-done.3, ...), kind=kOutput, calls=%fused_computation.22 | convolution fusion | flops 677117952 | bytes 9618432 | tf_op jit(solution)/shard_map/mnh,hc->mcn/dot_general | solution.py:113
  130.2 1.6 copy.117
  131.8 1.6 reshape.333
  133.4 3.7 %all-to-all-start = ((bf16[4,2,32768]{2,1,0:T(2,128)(2,1)}), bf16[4,2,32768]{2,1,0:T(2,128)(2,1)S(1)}, u32[]{:S(2)}, u32[]{:S(2)}) async-start(bf16[4,2,32768]{2,1,0:T(2,128)(2,1)} %reshape.333), calls=%async_computation | async-start | bytes 1048576 | tf_op jit(solution)/shard_map/all_to_all | solution.py:120
  137.9 7.3 %all-to-all-done = bf16[4,2,32768]{2,1,0:T(2,128)(2,1)S(1)} async-done(((bf16[4,2,32768]{2,1,0:T(2,128)(2,1)}), bf16[4,2,32768]{2,1,0:T(2,128)(2,1)S(1)}, u32[]{:S(2)}, u32[]{:S(2)}) %all-to-all-start) | async-done | bytes 524320 | tf_op jit(solution)/shard_map/all_to_all | solution.py:120
  147.4 2.7 %copy.122 = f32[4,32,64,32]{3,2,1,0:T(8,128)} copy(f32[4,32,64,32]{2,3,0,1:T(8,128)S(1)} %bitcast.166) | data formatting | bytes 2097152 | tf_op jit(solution)/shard_map/convert_element_type | solution.py:124
  150.2 3.6 %reshape.264 = f32[128,2048]{1,0:T(8,128)S(1)} reshape(f32[4,32,64,32]{3,2,1,0:T(8,128)} %copy.122) | data formatting | bytes 2097152 | tf_op jit(solution)/shard_map/convert_element_type | solution.py:124
  155.5 1.7 copy.124
  158.1 13.2 %all_to_all.27 = bf16[4,2,32768]{2,1,0:T(2,128)(2,1)S(1)} all-to-all(bf16[4,2,32768]{2,1,0:T(2,128)(2,1)S(1)} %reshape.335), channel_id=1, replica_groups=mesh['member'=4,'space'=128] {'member'}, dimensions={0} | all-to-all | bytes 1048576 | tf_op jit(solution)/shard_map/all_to_all | solution.py:160
  (86 shorter events, 18.0 us)
Async XLA Ops:
  0.0 111.5 %copy-start = (bf16[1,256,256]{2,1,0:T(8,128)(2,1)S(1)}, bf16[1,256,256]{2,1,0:T(8,128)(2,1)}, u32[]{:S(2)}) copy-start(bf16[1,256,256]{2,1,0:T(8,128)(2,1)} %param.17) | copy-start | bytes 393220
  0.0 31.1 %copy-start.4 = (bf16[1,256,256]{2,1,0:T(8,128)(2,1)S(1)}, bf16[1,256,256]{2,1,0:T(8,128)(2,1)}, u32[]{:S(2)}) copy-start(bf16[1,256,256]{2,1,0:T(8,128)(2,1)} %param.16) | copy-start | bytes 393220
  0.0 34.5 %collective-permute-start.1 = (s32[2,32]{1,0:T(2,128)}, s32[2,32]{1,0:T(2,128)S(1)}, u32[]{:S(2)}, u32[]{:S(2)}) collective-permute-start(s32[2,32]{1,0:T(2,128)} %param.22), channel_id=1, source_target_pairs={{1,0},{2,1},{3,2},{4,3},{5,4},{6,5},{7,6},{8,7},{9,8},{10,9},{11,1... | collective-permute-start | bytes 776 | tf_op jit(solution)/shard_map/ppermute | solution.py:22
  17.1 17.5 %collective-permute-start = (s32[2,32]{1,0:T(2,128)}, s32[2,32]{1,0:T(2,128)S(1)}, u32[]{:S(2)}, u32[]{:S(2)}) collective-permute-start(s32[2,32]{1,0:T(2,128)} %param.22), channel_id=1, source_target_pairs={{0,1},{1,2},{2,3},{3,4},{4,5},{5,6},{6,7},{7,8},{8,9},{9,10},{10,1... | collective-permute-start | bytes 776 | tf_op jit(solution)/shard_map/ppermute | solution.py:20
  22.6 15.0 %collective-permute-start.5 = (f32[1,1,129,128]{3,2,1,0:T(8,128)S(1)}, f32[1,1,129,128]{3,2,1,0:T(8,128)S(1)}, u32[]{:S(2)}, u32[]{:S(2)}) collective-permute-start(f32[1,1,129,128]{3,2,1,0:T(8,128)S(1)} %maximum_bitcast_fusion), channel_id=1, source_target_pairs={{128,0},{256,128},{384,256},{0,384},{129,1},{257,129},{385,257},{1... | collective-permute-start | bytes 198152 | tf_op jit(solution)/shard_map/ppermute | solution.py:22
  25.8 11.8 %collective-permute-start.4 = (f32[1,1,129,128]{3,2,1,0:T(8,128)S(1)}, f32[1,1,129,128]{3,2,1,0:T(8,128)S(1)}, u32[]{:S(2)}, u32[]{:S(2)}) collective-permute-start(f32[1,1,129,128]{3,2,1,0:T(8,128)S(1)} %maximum_bitcast_fusion), channel_id=1, source_target_pairs={{0,128},{128,256},{256,384},{384,0},{1,129},{129,257},{257,385},{3... | collective-permute-start | bytes 198152 | tf_op jit(solution)/shard_map/ppermute | solution.py:20
  31.1 3.4 %copy-start.1 = (f32[32,128,256]{2,1,0:T(8,128)}, f32[32,128,256]{2,1,0:T(8,128)S(1)}, u32[]{:S(2)}) copy-start(f32[32,128,256]{2,1,0:T(8,128)S(1)} %fusion.40) | copy-start | bytes 12582916
  31.1 0.8 copy-start.7
  31.1 3.4 %copy-start.6 = (bf16[1,256]{1,0:T(2,128)(2,1)S(1)}, bf16[1,256]{1,0:T(2,128)(2,1)}, u32[]{:S(2)}) copy-start(bf16[1,256]{1,0:T(2,128)(2,1)} %param.19) | copy-start | bytes 1540
  37.6 18.5 %collective-permute-start.7 = (f32[3,1,129,128]{3,2,1,0:T(8,128)S(1)}, f32[3,1,129,128]{3,2,1,0:T(8,128)S(1)}, u32[]{:S(2)}, u32[]{:S(2)}) collective-permute-start(f32[3,1,129,128]{3,2,1,0:T(8,128)S(1)} %pad_maximum_fusion.3), channel_id=1, source_target_pairs={{1,0},{2,1},{3,2},{4,3},{5,4},{6,5},{7,6},{8,7},{9,8},{10,9},{11,1... | collective-permute-start | bytes 594440 | tf_op jit(solution)/shard_map/ppermute | solution.py:22
  49.9 49.5 %collective-permute-start.3 = (bf16[32,32,256]{2,1,0:T(8,128)(2,1)}, bf16[32,32,256]{2,1,0:T(8,128)(2,1)}, u32[]{:S(2)}, u32[]{:S(2)}) collective-permute-start(bf16[32,32,256]{2,1,0:T(8,128)(2,1)} %get-tuple-element.18), channel_id=1, source_target_pairs={{1,0},{2,1},{3,2},{4,3},{5,4},{6,5},{7,6},{8,7},{9,8},{10,9},{11,1... | collective-permute-start | bytes 1572872 | tf_op jit(solution)/shard_map/ppermute | solution.py:22
  51.8 47.6 %collective-permute-start.2 = (bf16[32,32,256]{2,1,0:T(8,128)(2,1)}, bf16[32,32,256]{2,1,0:T(8,128)(2,1)}, u32[]{:S(2)}, u32[]{:S(2)}) collective-permute-start(bf16[32,32,256]{2,1,0:T(8,128)(2,1)} %get-tuple-element.17), channel_id=1, source_target_pairs={{0,1},{1,2},{2,3},{3,4},{4,5},{5,6},{6,7},{7,8},{8,9},{9,10},{10,1... | collective-permute-start | bytes 1572872 | tf_op jit(solution)/shard_map/ppermute | solution.py:20
  54.2 26.5 %collective-permute-start.6 = (f32[3,1,129,128]{3,2,1,0:T(8,128)S(1)}, f32[3,1,129,128]{3,2,1,0:T(8,128)S(1)}, u32[]{:S(2)}, u32[]{:S(2)}) collective-permute-start(f32[3,1,129,128]{3,2,1,0:T(8,128)S(1)} %pad_maximum_fusion.3), channel_id=1, source_target_pairs={{0,1},{1,2},{2,3},{3,4},{4,5},{5,6},{6,7},{7,8},{8,9},{9,10},{10,1... | collective-permute-start | bytes 594440 | tf_op jit(solution)/shard_map/ppermute | solution.py:20
  56.2 26.5 %collective-permute-start.9 = (bf16[1,129,128]{2,1,0:T(8,128)(2,1)S(1)}, bf16[1,129,128]{2,1,0:T(8,128)(2,1)S(1)}, u32[]{:S(2)}, u32[]{:S(2)}) collective-permute-start(bf16[1,129,128]{2,1,0:T(8,128)(2,1)S(1)} %fusion.37), channel_id=1, source_target_pairs={{1,0},{2,1},{3,2},{4,3},{5,4},{6,5},{7,6},{8,7},{9,8},{10,9},{11,1... | collective-permute-start | bytes 99080 | tf_op jit(solution)/shard_map/ppermute | solution.py:22
  80.8 13.4 %collective-permute-start.8 = (bf16[1,129,128]{2,1,0:T(8,128)(2,1)S(1)}, bf16[1,129,128]{2,1,0:T(8,128)(2,1)S(1)}, u32[]{:S(2)}, u32[]{:S(2)}) collective-permute-start(bf16[1,129,128]{2,1,0:T(8,128)(2,1)S(1)} %fusion.36), channel_id=1, source_target_pairs={{0,1},{1,2},{2,3},{3,4},{4,5},{5,6},{6,7},{7,8},{8,9},{9,10},{10,1... | collective-permute-start | bytes 99080 | tf_op jit(solution)/shard_map/ppermute | solution.py:20
  111.5 13.8 %copy-start.2 = (bf16[32,64,128]{2,1,0:T(8,128)(2,1)S(1)}, bf16[32,64,128]{2,1,0:T(8,128)(2,1)}, u32[]{:S(2)}) copy-start(bf16[32,64,128]{2,1,0:T(8,128)(2,1)} %param.14) | copy-start | bytes 1572868
  111.5 13.8 %copy-start.3 = (bf16[1,256,256]{2,1,0:T(8,128)(2,1)S(1)}, bf16[1,256,256]{2,1,0:T(8,128)(2,1)}, u32[]{:S(2)}) copy-start(bf16[1,256,256]{2,1,0:T(8,128)(2,1)} %param.18) | copy-start | bytes 393220
  111.5 13.8 %copy-start.5 = (bf16[256,64]{0,1:T(8,128)(2,1)S(1)}, bf16[256,64]{0,1:T(8,128)(2,1)}, u32[]{:S(2)}) copy-start(bf16[256,64]{0,1:T(8,128)(2,1)} %param.20) | copy-start | bytes 98308
  133.4 11.8 %all-to-all-start = ((bf16[4,2,32768]{2,1,0:T(2,128)(2,1)}), bf16[4,2,32768]{2,1,0:T(2,128)(2,1)S(1)}, u32[]{:S(2)}, u32[]{:S(2)}) async-start(bf16[4,2,32768]{2,1,0:T(2,128)(2,1)} %reshape.333), calls=%async_computation | async-start | bytes 1048576 | tf_op jit(solution)/shard_map/all_to_all | solution.py:120
where the time goes:
time: 174 us; the launch traced here: 173 us
  starting transfers between devices  59.6 us (34%)
  local copies, waits for them, and re-layouts  33.2 us (19%)
  waiting for transfers between devices  31.5 us (18%)
  matrix products  28.9 us (17%)
  blocking collectives  13.2 us (8%)
  other arithmetic  5.66 us (3%)
    ppermute x5, starting transfers between devices, extended_2(): lax.ppermute(head, axis, [((i + 1) % count, i) for i in range(count)])  45.2 us
    ppermute x5, waiting for transfers between devices, extended_2(): lax.ppermute(tail, axis, [(i, (i + 1) % count) for i in range(count)])  24.2 us
    dot_general x1, matrix products, body(): jnp.einsum('mnh,hk->mnk', rounded, receive_weight[0], preferred_element_t...  13.8 us
    all_to_all x1, blocking collectives, body(): lax.all_to_all(analysed, 'member', split_axis=0, concat_axis=2, tiled=True)  13.2 us
    ppermute x5, starting transfers between devices, extended_2(): lax.ppermute(tail, axis, [(i, (i + 1) % count) for i in range(count)])  10.7 us
    gather x4, local copies, waits for them, and re-layouts, body(): sender_rows = jnp.take(extended, edge_senders[:, slot_index], axis=1)  8.04 us
    all_to_all x1, waiting for transfers between devices, body(): lax.all_to_all(predicted_fields, 'member', split_axis=2, concat_axis=0, t...  7.27 us
    convert_element_type x3, local copies, waits for them, and re-layouts, body(): states = regional_states.reshape(ensemble, -1).astype(jnp.float32)  6.73 us
  transfers between devices with their start and end apart: 11, of which 3 were waited for; matrix products, arithmetic and copies ran while one was open for 11% of the time, Pallas kernels for 0%

commit v1 on v0

v1 whole, which is shorter than its diff:
```python
import functools

import jax
import jax.numpy as jnp
from jax import lax
from jax.experimental import pallas as pl
from jax.experimental.pallas import tpu as pltpu
from jax.sharding import PartitionSpec as P

ITERS_NS = 5
EPSILON = 1e-05
FULL_PRECISION = lax.Precision.HIGHEST
MESH = pl.DeviceIdType.MESH
BF16 = jnp.bfloat16
F32 = jnp.float32

MEMBERS = 32
CHANNELS = 64
NODES = 128
HIDDEN = 256
HALO = 32
SLOTS = 4
PARTS = 4
ENSEMBLE = 128
GRAM_ROWS = 144
MEMBER_CHUNKS = 2
CHANNEL_CHUNKS = 4


def dot(left, right):
    return jnp.dot(left, right, preferred_element_type=F32)


def dot_nt(left, right):
    return lax.dot_general(left, right, (((1,), (1,)), ((), ())), preferred_element_type=F32)


def iota(shape, dim):
    return lax.broadcasted_iota(jnp.int32, shape, dim)


def eye(extent, dtype):
    return jnp.where(iota((extent, extent), 0) == iota((extent, extent), 1), 1.0, 0.0).astype(dtype)


def split(values):
    high = values.astype(BF16)
    return high, (values - high.astype(F32)).astype(BF16)


def kernel(
    member_count,
    space_count,
    fields_hbm,
    we_ref,
    ws_ref,
    wr_ref,
    wu_ref,
    gain_ref,
    wd_ref,
    edge_ref,
    halo_ref,
    pert_ref,
    vals_ref,
    near_ref,
    out_ref,
    fv,
    we_t,
    wsr_t,
    wu_t,
    wd_t,
    gain_col,
    pick,
    perm,
    perm_halo,
    lists,
    nears,
    halo_send,
    halo_recv,
    se,
    rv,
    sh,
    vs,
    ms,
    nb,
    fs,
    sb,
    xr,
    zs,
    zr,
    os_,
    gram_own,
    gram_send,
    gram_member,
    sum_send,
    sum_recv,
    gram_far,
    field_sem,
    list_send_sem,
    list_recv_sem,
    near_send_sem,
    near_recv_sem,
    halo_send_sem,
    halo_recv_sem,
    gm_send_sem,
    gm_recv_sem,
    sum_send_sem,
    sum_recv_sem,
    far_send_sem,
    far_recv_sem,
    x_send_sem,
    x_recv_sem,
    z_send_sem,
    z_recv_sem,
):
    row = lax.axis_index("member")
    column = lax.axis_index("space")

    def at_member(offset):
        return (lax.rem(row + offset + member_count, member_count), column)

    def at_space(offset):
        return (row, lax.rem(column + offset + space_count, space_count))

    def remote(source, target, send_sem, recv_sem, device):
        return pltpu.make_async_remote_copy(
            src_ref=source,
            dst_ref=target,
            send_sem=send_sem,
            recv_sem=recv_sem,
            device_id=device,
            device_id_type=MESH,
        )

    load_fields = pltpu.make_async_copy(fields_hbm, fv, field_sem)
    load_fields.start()
    barrier = pltpu.get_barrier_semaphore()
    partners = [at_space(-1), at_space(1), at_space(-2), at_space(2)]
    partners += [at_member(d) for d in range(1, PARTS)]
    for partner in partners:
        pl.semaphore_signal(barrier, inc=1, device_id=partner, device_id_type=MESH)

    pert = pert_ref[0]
    variance = vals_ref[0, 0:1, :].astype(F32)
    innovation = vals_ref[0, 1:2, :].astype(F32)
    scaled_high, scaled_low = split(pert.astype(F32) * variance)
    gram = dot_nt(scaled_high, pert) + dot_nt(scaled_low, pert)
    force_high, force_low = split(variance * innovation)
    sub = iota((16, HIDDEN), 0)
    force_rows = jnp.where(
        sub == 0,
        jnp.broadcast_to(force_high.astype(F32), (16, HIDDEN)),
        jnp.where(sub == 1, jnp.broadcast_to(force_low.astype(F32), (16, HIDDEN)), 0.0),
    ).astype(BF16)
    forcing = jnp.sum(dot_nt(force_rows, pert), axis=0, keepdims=True)
    sub16 = iota((16, ENSEMBLE), 0)

    def forcing_rows(values):
        high = values.astype(BF16).astype(F32)
        low = values - high
        return jnp.where(
            sub16 == 0,
            jnp.broadcast_to(high, (16, ENSEMBLE)),
            jnp.where(sub16 == 1, jnp.broadcast_to(low, (16, ENSEMBLE)), 0.0),
        )

    gram_own[0:ENSEMBLE, :] = gram
    gram_own[ENSEMBLE:GRAM_ROWS, :] = forcing_rows(forcing)
    gram_send[...] = gram_own[...].astype(BF16)

    pl.semaphore_wait(barrier, len(partners))

    list_copies = []
    for i, offset in enumerate((1, -1)):
        list_copies.append(
            remote(halo_ref, lists.at[i], list_send_sem.at[i], list_recv_sem.at[i], at_space(offset))
        )
        list_copies.append(
            remote(near_ref, nears.at[i], near_send_sem.at[i], near_recv_sem.at[i], at_space(offset))
        )
    for copy in list_copies:
        copy.start()
    member_copies = [
        remote(gram_send, gram_member.at[i], gm_send_sem.at[i], gm_recv_sem.at[i], at_member(offset))
        for i, offset in enumerate((1, -1))
    ]
    far_copies = [
        remote(gram_send, gram_far.at[i], far_send_sem.at[i], far_recv_sem.at[i], at_space(offset))
        for i, offset in enumerate((2, -2))
    ]
    for copy in member_copies:
        copy.start()

    eye_hidden = eye(HIDDEN, BF16)
    we_t[...] = dot_nt(eye_hidden, we_ref[...]).astype(BF16)
    wsr_t[0:HIDDEN, :] = dot_nt(eye_hidden, ws_ref[0]).astype(BF16)
    wsr_t[HIDDEN:, :] = (dot_nt(eye_hidden, wr_ref[0]) * 0.5).astype(BF16)

    load_fields.wait()
    for i in range(2):
        list_copies[2 * i].wait_recv()

    repeat = jnp.where(
        iota((HALO, NODES), 0) == (iota((HALO, NODES), 1) & (HALO - 1)), 1.0, 0.0
    ).astype(BF16)
    node = iota((NODES, HALO), 0)
    block = iota((NODES, NODES), 1) >> 5
    wanted = []
    for names in (lists[1, 0:1, :], lists[0, 1:2, :]):
        one_hot = jnp.where(node == jnp.broadcast_to(names, (NODES, HALO)), 1.0, 0.0).astype(BF16)
        wanted.append(dot(one_hot, repeat))
    chooser = jnp.concatenate(
        [
            jnp.concatenate([jnp.where(block == q, w, 0.0) for w in wanted], axis=1)
            for q in range(PARTS)
        ],
        axis=0,
    ).astype(BF16)
    groups = MEMBERS // PARTS
    quads = jnp.concatenate(
        [
            jnp.concatenate([fv[PARTS * g + q] for g in range(groups)], axis=0)
            for q in range(PARTS)
        ],
        axis=1,
    )
    chosen = dot(quads, chooser).astype(BF16)
    halo_send[0] = chosen[:, 0:NODES]
    halo_send[1] = chosen[:, NODES:]
    halo_copies = [
        remote(
            halo_send.at[i],
            halo_recv.at[i],
            halo_send_sem.at[i],
            halo_recv_sem.at[i],
            at_space(offset),
        )
        for i, offset in enumerate((1, -1))
    ]
    for copy in halo_copies:
        copy.start()
    for copy in far_copies:
        copy.start()

    def project(g, carry):
        wide = jnp.concatenate([fv[PARTS * g + q] for q in range(PARTS)], axis=1)
        rounded = dot(we_t[...], wide).astype(BF16)
        both = dot(wsr_t[...], rounded)
        for q in range(PARTS):
            se[PARTS * g + q] = both[0:HIDDEN, NODES * q : NODES * (q + 1)].astype(BF16)
            rv[PARTS * g + q] = both[HIDDEN:, NODES * q : NODES * (q + 1)]
        return carry

    lax.fori_loop(0, groups, project, 0)

    wu_t[...] = dot_nt(eye_hidden, wu_ref[0]).astype(BF16)
    wd_t[...] = dot_nt(eye(CHANNELS, BF16), wd_ref[...]).astype(BF16)
    gain_col[...] = dot_nt(eye_hidden, jnp.broadcast_to(gain_ref[...], (NODES, HIDDEN)))
    lane = iota((NODES, HIDDEN), 1)
    for k in range(SLOTS):
        sender = jnp.broadcast_to(edge_ref[:, k : k + 1], (NODES, HIDDEN))
        for i in range(2):
            moved = sender + jnp.where(sender >= NODES, 2 * HALO * i, 0)
            hot = jnp.where(lane == moved, 0.5, 0.0).astype(BF16)
            pick[i, :, NODES * k : NODES * (k + 1)] = dot_nt(eye_hidden, hot).astype(BF16)
    wide_lanes = PARTS * NODES
    r0 = iota((wide_lanes, wide_lanes), 0)
    goal = ((r0 >> 5) & 3) * NODES + (r0 >> 7) * HALO + (r0 & 31)
    perm[...] = jnp.where(iota((wide_lanes, wide_lanes), 1) == goal, 1.0, 0.0).astype(BF16)
    r1 = iota((HIDDEN, HIDDEN), 0)
    goal = ((r1 >> 5) & 3) * (2 * HALO) + (r1 >> 7) * HALO + (r1 & 31)
    perm_halo[...] = jnp.where(iota((HIDDEN, HIDDEN), 1) == goal, 1.0, 0.0).astype(BF16)

    def region(p, s):
        r = lax.rem(row + p + member_count, member_count)
        c = lax.rem(column + s + space_count, space_count)
        return r * space_count + c

    def weight(names, p, s, base):
        held = jnp.sum(
            jnp.where(names == region(p, base + s), 1.0, 0.0), axis=1, keepdims=True
        )
        return held * (1.0 / (1.0 + (p * p + s * s) / 2.0))

    for copy in member_copies:
        copy.wait_recv()
    for i in range(2):
        list_copies[2 * i + 1].wait_recv()
    rows = [(-1, gram_member[0].astype(F32)), (0, gram_own[...]), (1, gram_member[1].astype(F32))]
    for i, (offset, s) in enumerate(((1, -1), (-1, 1))):
        names = nears[1 - i]
        total = sum(weight(names, p, s, offset) * values for p, values in rows)
        sum_send[i, 0:ENSEMBLE, :] = total[0:ENSEMBLE].astype(BF16)
        sum_send[i, ENSEMBLE:, :] = forcing_rows(
            jnp.sum(total[ENSEMBLE:], axis=0, keepdims=True)
        ).astype(BF16)
    sum_copies = [
        remote(
            sum_send.at[i], sum_recv.at[i], sum_send_sem.at[i], sum_recv_sem.at[i], at_space(offset)
        )
        for i, offset in enumerate((1, -1))
    ]
    for copy in sum_copies:
        copy.start()

    for copy in halo_copies:
        copy.wait_recv()

    def project_halo(g, carry):
        at = pl.ds(pl.multiple_of(g * CHANNELS, CHANNELS), CHANNELS)
        both = jnp.concatenate([halo_recv[0, at, :], halo_recv[1, at, :]], axis=1)
        ordered = dot(both, perm_halo[...]).astype(BF16)
        rounded = dot(we_t[...], ordered).astype(BF16)
        values = dot(wsr_t[0:HIDDEN, :], rounded).astype(BF16)
        sh[2 * g] = values[:, 0:NODES]
        sh[2 * g + 1] = values[:, NODES:]
        return carry

    lax.fori_loop(0, groups, project_halo, 0)

    strip = 64

    def forecast(g, place):
        for i in range(2):
            left = jnp.concatenate(
                [
                    jnp.concatenate([se[PARTS * g + 2 * j + i], sh[2 * g + j]], axis=1)
                    for j in range(2)
                ],
                axis=0,
            )
            vs[...] = dot(left, pick[i])
            for j in range(2):
                square = jnp.zeros((8, NODES), F32)
                for top in range(0, HIDDEN, strip):
                    base = rv[PARTS * g + 2 * j + i, top : top + strip, :]
                    total = None
                    for k in range(SLOTS):
                        half = (
                            vs[
                                HIDDEN * j + top : HIDDEN * j + top + strip,
                                NODES * k : NODES * (k + 1),
                            ]
                            + base
                        )
                        term = half + half * jnp.tanh(half)
                        total = term if total is None else total + term
                    ms[top : top + strip, :] = total
                    squared = total * total
                    for t in range(0, strip, 8):
                        square = square + squared[t : t + 8]
                mean_square = jnp.sum(square, axis=0, keepdims=True) * (1.0 / HIDDEN)
                scale = lax.rsqrt(mean_square + EPSILON)
                q = 2 * j + i
                for top in range(0, HIDDEN, strip):
                    nb[top : top + strip, NODES * q : NODES * (q + 1)] = (
                        ms[top : top + strip, :] * scale * gain_col[top : top + strip, :]
                    ).astype(BF16)
        wide = jnp.concatenate([fv[PARTS * g + q] for q in range(PARTS)], axis=1)
        final = (dot(we_t[...], wide) + dot(wu_t[...], nb[...])).astype(BF16)
        values = dot(wd_t[...], final) + wide.astype(F32)
        for q in range(PARTS):
            fs[pl.ds(pl.multiple_of((place * PARTS + q) * CHANNELS, CHANNELS), CHANNELS), :] = (
                values[:, NODES * q : NODES * (q + 1)]
            )

    members = MEMBERS // MEMBER_CHUNKS
    x_copies = []
    for chunk in range(MEMBER_CHUNKS):
        steps = groups // MEMBER_CHUNKS

        def step(place, carry):
            forecast(chunk * steps + place, place)
            return carry

        lax.fori_loop(0, steps, step, 0)
        packed = jnp.concatenate(
            [
                jnp.concatenate(
                    [
                        fs[pl.ds(PARTS * cg + c, members, stride=CHANNELS), :]
                        for c in range(PARTS)
                    ],
                    axis=1,
                ).astype(BF16)
                for cg in range(CHANNELS // PARTS)
            ],
            axis=0,
        )
        turned = dot(packed, perm[...]).astype(BF16)
        for target in range(PARTS):
            sb[target, chunk] = turned[:, NODES * target : NODES * (target + 1)]
        for d in range(1, PARTS):
            device = at_member(d)
            copy = remote(
                sb.at[device[0], chunk],
                xr.at[row, chunk],
                x_send_sem.at[chunk, d - 1],
                x_recv_sem.at[chunk, d - 1],
                device,
            )
            copy.start()
            x_copies.append(copy)
        xr[row, chunk] = sb[row, chunk]

    for copy in sum_copies + far_copies:
        copy.wait_recv()
    names = near_ref[...]
    total = gram_own[...] + sum_recv[0].astype(F32) + sum_recv[1].astype(F32)
    for values, p, s in (
        (gram_member[0], -1, 0),
        (gram_member[1], 1, 0),
        (gram_far[0], 0, -2),
        (gram_far[1], 0, 2),
    ):
        total = total + weight(names, p, s, 0) * values.astype(F32)
    forcing = jnp.sum(total[ENSEMBLE:], axis=0, keepdims=True)
    identity = eye(ENSEMBLE, F32)
    system = identity + total[0:ENSEMBLE] / (ENSEMBLE - 1)
    norm = jnp.sum(jnp.sum(system * system, axis=1, keepdims=True), axis=0, keepdims=True)
    scaling = jnp.sqrt(norm)
    iterate = system / scaling
    inverse = identity

    def full(left, right):
        return jnp.dot(left, right, precision=FULL_PRECISION, preferred_element_type=F32)

    for _ in range(ITERS_NS):
        correction = 1.5 * identity - 0.5 * full(inverse, iterate)
        iterate = full(iterate, correction)
        inverse = full(correction, inverse)
    forcing = jnp.broadcast_to(forcing, (8, ENSEMBLE))
    mean_weights = full(full(forcing, inverse), inverse)[0:1] / (scaling * (ENSEMBLE - 1))
    root = inverse / jnp.sqrt(scaling)
    rest = (
        1.0
        - jnp.sum(root, axis=1, keepdims=True)
        - jnp.sum(mean_weights, axis=1, keepdims=True)
    ) * (1.0 / ENSEMBLE)
    mix_high, mix_low = split(root + mean_weights + rest)

    for copy in x_copies:
        copy.wait_recv()
    per_chunk = CHANNELS // PARTS // CHANNEL_CHUNKS
    owned = MEMBERS
    z_copies = []
    for ch in range(CHANNEL_CHUNKS):
        states = jnp.concatenate(
            [
                jnp.concatenate(
                    [
                        xr[source, chunk, members * cg : members * (cg + 1), :]
                        for source in range(PARTS)
                        for chunk in range(MEMBER_CHUNKS)
                    ],
                    axis=0,
                )
                for cg in range(ch * per_chunk, (ch + 1) * per_chunk)
            ],
            axis=1,
        )
        mixed = (dot(mix_high, states) + dot(mix_low, states)).astype(BF16)
        for target in range(PARTS):
            for cg in range(per_chunk):
                zs[target, ch, owned * cg : owned * (cg + 1), :] = mixed[
                    owned * target : owned * (target + 1), NODES * cg : NODES * (cg + 1)
                ]
        sent = []
        for d in range(1, PARTS):
            device = at_member(d)
            copy = remote(
                zs.at[device[0], ch],
                zr.at[row, ch],
                z_send_sem.at[ch, d - 1],
                z_recv_sem.at[ch, d - 1],
                device,
            )
            copy.start()
            sent.append(copy)
        z_copies.append(sent)
        zr[row, ch] = zs[row, ch]

    span = PARTS * per_chunk
    for ch in range(CHANNEL_CHUNKS):
        for copy in z_copies[ch]:
            copy.wait_recv()
        packed = jnp.concatenate([zr[source, ch] for source in range(PARTS)], axis=1)
        turned = dot(packed, perm[...])
        for cg in range(per_chunk):
            for c in range(PARTS):
                os_[pl.ds(PARTS * cg + c, owned, stride=span), :] = turned[
                    owned * cg : owned * (cg + 1), NODES * c : NODES * (c + 1)
                ]
        for j in range(owned):
            out_ref[j, span * ch : span * (ch + 1), :] = os_[span * j : span * (j + 1), :].astype(
                BF16
            )

    for copy in list_copies + member_copies + far_copies + halo_copies + sum_copies + x_copies:
        copy.wait_send()
    for sent in z_copies:
        for copy in sent:
            copy.wait_send()


def body(*arrays):
    vmem = pl.BlockSpec(memory_space=pltpu.VMEM)
    dma = pltpu.SemaphoreType.DMA
    return pl.pallas_call(
        functools.partial(kernel, lax.axis_size("member"), lax.axis_size("space")),
        out_shape=jax.ShapeDtypeStruct((MEMBERS, CHANNELS, NODES), BF16),
        in_specs=[pl.BlockSpec(memory_space=pl.ANY)] + [vmem] * 11,
        out_specs=vmem,
        scratch_shapes=[
            pltpu.VMEM((MEMBERS, CHANNELS, NODES), BF16),
            pltpu.VMEM((HIDDEN, CHANNELS), BF16),
            pltpu.VMEM((2 * HIDDEN, HIDDEN), BF16),
            pltpu.VMEM((HIDDEN, HIDDEN), BF16),
            pltpu.VMEM((CHANNELS, HIDDEN), BF16),
            pltpu.VMEM((HIDDEN, NODES), F32),
            pltpu.VMEM((2, HIDDEN, SLOTS * NODES), BF16),
            pltpu.VMEM((PARTS * NODES, PARTS * NODES), BF16),
            pltpu.VMEM((HIDDEN, HIDDEN), BF16),
            pltpu.VMEM((2, 2, HALO), jnp.int32),
            pltpu.VMEM((2, 1, 8), jnp.int32),
            pltpu.VMEM((2, MEMBERS // PARTS * CHANNELS, NODES), BF16),
            pltpu.VMEM((2, MEMBERS // PARTS * CHANNELS, NODES), BF16),
            pltpu.VMEM((MEMBERS, HIDDEN, NODES), BF16),
            pltpu.VMEM((MEMBERS, HIDDEN, NODES), F32),
            pltpu.VMEM((MEMBERS // 2, HIDDEN, NODES), BF16),
            pltpu.VMEM((2 * HIDDEN, SLOTS * NODES), F32),
            pltpu.VMEM((HIDDEN, NODES), F32),
            pltpu.VMEM((HIDDEN, PARTS * NODES), BF16),
            pltpu.VMEM((MEMBERS // MEMBER_CHUNKS * CHANNELS, NODES), F32),
            pltpu.VMEM((PARTS, MEMBER_CHUNKS, 256, NODES), BF16),
            pltpu.VMEM((PARTS, MEMBER_CHUNKS, 256, NODES), BF16),
            pltpu.VMEM((PARTS, CHANNEL_CHUNKS, 512 // CHANNEL_CHUNKS, NODES), BF16),
            pltpu.VMEM((PARTS, CHANNEL_CHUNKS, 512 // CHANNEL_CHUNKS, NODES), BF16),
            pltpu.VMEM((MEMBERS * CHANNELS // CHANNEL_CHUNKS, NODES), F32),
            pltpu.VMEM((GRAM_ROWS, ENSEMBLE), F32),
            pltpu.VMEM((GRAM_ROWS, ENSEMBLE), BF16),
            pltpu.VMEM((2, GRAM_ROWS, ENSEMBLE), BF16),
            pltpu.VMEM((2, GRAM_ROWS, ENSEMBLE), BF16),
            pltpu.VMEM((2, GRAM_ROWS, ENSEMBLE), BF16),
            pltpu.VMEM((2, GRAM_ROWS, ENSEMBLE), BF16),
            dma,
            dma((2,)),
            dma((2,)),
            dma((2,)),
            dma((2,)),
            dma((2,)),
            dma((2,)),
            dma((2,)),
            dma((2,)),
            dma((2,)),
            dma((2,)),
            dma((2,)),
            dma((2,)),
            dma((MEMBER_CHUNKS, PARTS - 1)),
            dma((MEMBER_CHUNKS, PARTS - 1)),
            dma((CHANNEL_CHUNKS, PARTS - 1)),
            dma((CHANNEL_CHUNKS, PARTS - 1)),
        ],
        compiler_params=pltpu.CompilerParams(collective_id=0, has_side_effects=True),
        name="cycle",
    )(*arrays)


def solution(mesh):
    placed = (
        P("member", None, "space"),
        P(),
        P(),
        P(),
        P(),
        P(),
        P(),
        P("space", None),
        P(None, "space"),
        P(("member", "space"), None, None),
        P(("member", "space"), None, None),
        P(("member", "space"), None),
    )
    return jax.shard_map(
        body, mesh=mesh, in_specs=placed, out_specs=P("member", None, "space"), check_vma=False
    )
```

time: 174 us -> 68.5 us (0.39)
  Pallas kernels: 0 us -> 64.1 us
  starting transfers between devices: 59.6 us -> 0 us
  waiting for transfers between devices: 31.5 us -> 0 us
  local copies, waits for them, and re-layouts: 33.2 us -> 4.12 us
  matrix products: 28.9 us -> 0 us
  blocking collectives: 13.2 us -> 0 us
  other arithmetic: 5.66 us -> 0 us
    pallas_call x0 -> x1, Pallas kernels: none -> 64.1 us  [body(): pl.pallas_call(functools.partial(kernel, lax.axis_size('member'), lax.axi...]
    ppermute x10 -> x0, starting transfers between devices: 55.9 us -> none  [the longest x5 45.2 us: extended_2(): lax.ppermute(head, axis, [((i + 1) % count, i) for i in range(count)])]
    dot_general x25 -> x0, matrix products: 28.9 us -> none  [the longest x1 13.8 us: body(): jnp.einsum('mnh,hk->mnk', rounded, receive_weight[0], preferred_element_t...]
    ppermute x10 -> x0, waiting for transfers between devices: 24.2 us -> none  [the longest x5 24.2 us: extended_2(): lax.ppermute(tail, axis, [(i, (i + 1) % count) for i in range(count)])]
    all_to_all x1 -> x0, blocking collectives: 13.2 us -> none  [body(): lax.all_to_all(analysed, 'member', split_axis=0, concat_axis=2, tiled=True)]
    convert_element_type x6 -> x0, local copies, waits for them, and re-layouts: 11.1 us -> none  [the longest x3 6.73 us: body(): states = regional_states.reshape(ensemble, -1).astype(jnp.float32)]
    gather x5 -> x0, local copies, waits for them, and re-layouts: 10.2 us -> none  [the longest x4 8.04 us: body(): sender_rows = jnp.take(extended, edge_senders[:, slot_index], axis=1)]
    all_to_all x1 -> x0, waiting for transfers between devices: 7.27 us -> none  [body(): lax.all_to_all(predicted_fields, 'member', split_axis=2, concat_axis=0, t...]
  transfers between devices with their start and end apart: 11 -> 0, of which waited for: 3 -> 0; matrix products, arithmetic and copies ran while one was open for 11% -> 0% of each run, Pallas kernels for 0% -> 0%
where the time goes in v1:
time: 68.5 us; the launch traced here: 68.2 us
  Pallas kernels  64.1 us (94%)
  local copies, waits for them, and re-layouts  4.12 us (6%)
    pallas_call x1, Pallas kernels, body(): pl.pallas_call(functools.partial(kernel, lax.axis_size('member'), lax.axi...  64.1 us
    unnamed x5, local copies, waits for them, and re-layouts  4.12 us

profile of v1, /device:TPU:8, one launch (start us, length us, event | category | flops | bytes accessed | tf_op | source)
XLA Modules:
  0.0 68.2 jit_solution(500669212756639625)
XLA Ops:
  0.0 0.0 copy-start
  0.0 1.5 %copy.13.wd_ref = bf16[256,64]{1,0:T(8,128)(2,1)} copy(bf16[256,64]{0,1:T(8,128)(2,1)} %param.18) | data formatting | bytes 65536 | tf_op args[6]
  1.5 0.0 copy-done
  1.5 0.7 %copy.14.edge_ref = s32[128,4]{1,0:T(8,128)} copy(s32[128,4]{0,1:T(4,128)S(1)} %copy-done) | data formatting | bytes 4096 | tf_op args[7]
  2.3 64.1 %cycle.1 = bf16[32,64,128]{2,1,0:T(8,128)(2,1)} custom-call(bf16[32,64,128]{2,1,0:T(8,128)(2,1)} %fields_hbm.1, bf16[64,256]{1,0:T(8,128)(2,1)} %we_ref.1, bf16[1,256,256]{2,1,0:T(8,128)(2,1)} %ws_ref.1, bf16[1,256,256]{2,1,0:T(8,128)(2,1)} %wr_ref.1, bf16[1,256,256]{2,1,0:T(8,128)(2,1)} %wu_ref.1, bf16[1,256]{1,0:T(2,128)(2,1)} %gain_ref.1, ...), custom_call_target="tpu_custom_call" | custom-call | tf_op jit(solution)/shard_map/cycle/pallas_call | solution.py:509
  66.3 1.9 %copy.16 = bf16[32,64,128]{2,1,0:T(8,128)(2,1)} copy(bf16[32,64,128]{2,1,0:T(8,128)(2,1)} %cycle.1) | data formatting | bytes 1048576
Async XLA Ops:
  0.0 1.5 %copy-start = (s32[128,4]{0,1:T(4,128)S(1)}, s32[128,4]{0,1:T(4,128)}, u32[]{:S(2)}) copy-start(s32[128,4]{0,1:T(4,128)} %param.19) | copy-start | bytes 6148

commit v2 on v1

--- a/solution.py
+++ b/solution.py
@@ -23,8 +23,10 @@
 PARTS = 4
 ENSEMBLE = 128
 GRAM_ROWS = 144
-MEMBER_CHUNKS = 2
+MEMBER_CHUNKS = 4
 CHANNEL_CHUNKS = 4
+HALO_STEP = 8
+OWN_STEP = 16
 
 
 def dot(left, right):
@@ -52,23 +54,33 @@
     member_count,
     space_count,
     fields_hbm,
+    we_hbm,
+    ws_hbm,
+    wr_hbm,
+    wu_hbm,
+    gain_hbm,
+    wd_hbm,
+    edge_hbm,
+    halo_hbm,
+    pert_hbm,
+    vals_hbm,
+    near_hbm,
+    out_ref,
+    fv,
     we_ref,
     ws_ref,
     wr_ref,
     wu_ref,
     gain_ref,
-    wd_ref,
+    wd_t,
     edge_ref,
     halo_ref,
     pert_ref,
     vals_ref,
     near_ref,
-    out_ref,
-    fv,
     we_t,
     wsr_t,
     wu_t,
-    wd_t,
     gain_col,
     pick,
     perm,
@@ -95,7 +107,7 @@
     sum_send,
     sum_recv,
     gram_far,
-    field_sem,
+    load_sem,
     list_send_sem,
     list_recv_sem,
     near_send_sem,
@@ -132,14 +144,33 @@
             device_id_type=MESH,
         )
 
-    load_fields = pltpu.make_async_copy(fields_hbm, fv, field_sem)
-    load_fields.start()
     barrier = pltpu.get_barrier_semaphore()
     partners = [at_space(-1), at_space(1), at_space(-2), at_space(2)]
     partners += [at_member(d) for d in range(1, PARTS)]
     for partner in partners:
         pl.semaphore_signal(barrier, inc=1, device_id=partner, device_id_type=MESH)
 
+    sources = (halo_hbm, near_hbm, pert_hbm, vals_hbm, we_hbm, ws_hbm, wr_hbm, fields_hbm)
+    sources += (edge_hbm, wu_hbm, gain_hbm, wd_hbm)
+    targets = (halo_ref, near_ref, pert_ref, vals_ref, we_ref, ws_ref, wr_ref, fv)
+    targets += (edge_ref, wu_ref, gain_ref, wd_t)
+    loads = [
+        pltpu.make_async_copy(source, target, load_sem.at[i])
+        for i, (source, target) in enumerate(zip(sources, targets))
+    ]
+    for load in loads:
+        load.start()
+
+    eye_hidden = eye(HIDDEN, BF16)
+    r1 = iota((HIDDEN, HIDDEN), 0)
+    goal = ((r1 >> 5) & 3) * (2 * HALO) + (r1 >> 7) * HALO + (r1 & 31)
+    perm_halo[...] = jnp.where(iota((HIDDEN, HIDDEN), 1) == goal, 1.0, 0.0).astype(BF16)
+    repeat = jnp.where(
+        iota((HALO, NODES), 0) == (iota((HALO, NODES), 1) & (HALO - 1)), 1.0, 0.0
+    ).astype(BF16)
+
+    for load in loads[0:4]:
+        load.wait()
     pert = pert_ref[0]
     variance = vals_ref[0, 0:1, :].astype(F32)
     innovation = vals_ref[0, 1:2, :].astype(F32)
@@ -191,18 +222,15 @@
     for copy in member_copies:
         copy.start()
 
-    eye_hidden = eye(HIDDEN, BF16)
+    for load in loads[4:]:
+        load.wait()
     we_t[...] = dot_nt(eye_hidden, we_ref[...]).astype(BF16)
     wsr_t[0:HIDDEN, :] = dot_nt(eye_hidden, ws_ref[0]).astype(BF16)
     wsr_t[HIDDEN:, :] = (dot_nt(eye_hidden, wr_ref[0]) * 0.5).astype(BF16)
 
-    load_fields.wait()
     for i in range(2):
         list_copies[2 * i].wait_recv()
 
-    repeat = jnp.where(
-        iota((HALO, NODES), 0) == (iota((HALO, NODES), 1) & (HALO - 1)), 1.0, 0.0
-    ).astype(BF16)
     node = iota((NODES, HALO), 0)
     block = iota((NODES, NODES), 1) >> 5
     wanted = []
@@ -242,34 +270,27 @@
     for copy in far_copies:
         copy.start()
 
-    def project(g, carry):
-        wide = jnp.concatenate([fv[PARTS * g + q] for q in range(PARTS)], axis=1)
+    for m in range(0, MEMBERS, OWN_STEP):
+        wide = jnp.concatenate([fv[m + t] for t in range(OWN_STEP)], axis=1)
         rounded = dot(we_t[...], wide).astype(BF16)
         both = dot(wsr_t[...], rounded)
-        for q in range(PARTS):
-            se[PARTS * g + q] = both[0:HIDDEN, NODES * q : NODES * (q + 1)].astype(BF16)
-            rv[PARTS * g + q] = both[HIDDEN:, NODES * q : NODES * (q + 1)]
-        return carry
-
-    lax.fori_loop(0, groups, project, 0)
+        for t in range(OWN_STEP):
+            se[m + t] = both[0:HIDDEN, NODES * t : NODES * (t + 1)].astype(BF16)
+            rv[m + t] = both[HIDDEN:, NODES * t : NODES * (t + 1)]
 
     wu_t[...] = dot_nt(eye_hidden, wu_ref[0]).astype(BF16)
-    wd_t[...] = dot_nt(eye(CHANNELS, BF16), wd_ref[...]).astype(BF16)
     gain_col[...] = dot_nt(eye_hidden, jnp.broadcast_to(gain_ref[...], (NODES, HIDDEN)))
-    lane = iota((NODES, HIDDEN), 1)
+    tall = iota((HIDDEN, NODES), 0)
     for k in range(SLOTS):
-        sender = jnp.broadcast_to(edge_ref[:, k : k + 1], (NODES, HIDDEN))
+        sender = jnp.broadcast_to(edge_ref[k : k + 1, :], (HIDDEN, NODES))
         for i in range(2):
             moved = sender + jnp.where(sender >= NODES, 2 * HALO * i, 0)
-            hot = jnp.where(lane == moved, 0.5, 0.0).astype(BF16)
-            pick[i, :, NODES * k : NODES * (k + 1)] = dot_nt(eye_hidden, hot).astype(BF16)
+            hot = jnp.where(tall == moved, 0.5, 0.0).astype(BF16)
+            pick[i, :, NODES * k : NODES * (k + 1)] = hot
     wide_lanes = PARTS * NODES
     r0 = iota((wide_lanes, wide_lanes), 0)
     goal = ((r0 >> 5) & 3) * NODES + (r0 >> 7) * HALO + (r0 & 31)
     perm[...] = jnp.where(iota((wide_lanes, wide_lanes), 1) == goal, 1.0, 0.0).astype(BF16)
-    r1 = iota((HIDDEN, HIDDEN), 0)
-    goal = ((r1 >> 5) & 3) * (2 * HALO) + (r1 >> 7) * HALO + (r1 & 31)
-    perm_halo[...] = jnp.where(iota((HIDDEN, HIDDEN), 1) == goal, 1.0, 0.0).astype(BF16)
 
     def region(p, s):
         r = lax.rem(row + p + member_count, member_count)
@@ -306,21 +327,22 @@
     for copy in halo_copies:
         copy.wait_recv()
 
-    def project_halo(g, carry):
-        at = pl.ds(pl.multiple_of(g * CHANNELS, CHANNELS), CHANNELS)
-        both = jnp.concatenate([halo_recv[0, at, :], halo_recv[1, at, :]], axis=1)
-        ordered = dot(both, perm_halo[...]).astype(BF16)
-        rounded = dot(we_t[...], ordered).astype(BF16)
+    both = jnp.concatenate([halo_recv[0], halo_recv[1]], axis=1)
+    ordered = dot(both, perm_halo[...]).astype(BF16)
+    for g in range(0, groups, HALO_STEP):
+        wide = jnp.concatenate(
+            [ordered[CHANNELS * t : CHANNELS * (t + 1)] for t in range(g, g + HALO_STEP)], axis=1
+        )
+        rounded = dot(we_t[...], wide).astype(BF16)
         values = dot(wsr_t[0:HIDDEN, :], rounded).astype(BF16)
-        sh[2 * g] = values[:, 0:NODES]
-        sh[2 * g + 1] = values[:, NODES:]
-        return carry
-
-    lax.fori_loop(0, groups, project_halo, 0)
+        for t in range(2 * HALO_STEP):
+            sh[2 * g + t] = values[:, NODES * t : NODES * (t + 1)]
 
     strip = 64
-
-    def forecast(g, place):
+    members = MEMBERS // MEMBER_CHUNKS
+    x_copies = []
+
+    def gather(g):
         for i in range(2):
             left = jnp.concatenate(
                 [
@@ -329,15 +351,21 @@
                 ],
                 axis=0,
             )
-            vs[...] = dot(left, pick[i])
+            vs[g % 2, i] = dot(left, pick[i])
+
+    def message(g):
+        for i in range(2):
             for j in range(2):
+                q = 2 * j + i
                 square = jnp.zeros((8, NODES), F32)
                 for top in range(0, HIDDEN, strip):
-                    base = rv[PARTS * g + 2 * j + i, top : top + strip, :]
+                    base = rv[PARTS * g + q, top : top + strip, :]
                     total = None
                     for k in range(SLOTS):
                         half = (
                             vs[
+                                g % 2,
+                                i,
                                 HIDDEN * j + top : HIDDEN * j + top + strip,
                                 NODES * k : NODES * (k + 1),
                             ]
@@ -345,48 +373,40 @@
                         )
                         term = half + half * jnp.tanh(half)
                         total = term if total is None else total + term
-                    ms[top : top + strip, :] = total
+                    ms[q, top : top + strip, :] = total
                     squared = total * total
                     for t in range(0, strip, 8):
                         square = square + squared[t : t + 8]
                 mean_square = jnp.sum(square, axis=0, keepdims=True) * (1.0 / HIDDEN)
                 scale = lax.rsqrt(mean_square + EPSILON)
-                q = 2 * j + i
                 for top in range(0, HIDDEN, strip):
-                    nb[top : top + strip, NODES * q : NODES * (q + 1)] = (
-                        ms[top : top + strip, :] * scale * gain_col[top : top + strip, :]
+                    nb[g % 2, top : top + strip, NODES * q : NODES * (q + 1)] = (
+                        ms[q, top : top + strip, :] * scale * gain_col[top : top + strip, :]
                     ).astype(BF16)
+
+    def update(g):
         wide = jnp.concatenate([fv[PARTS * g + q] for q in range(PARTS)], axis=1)
-        final = (dot(we_t[...], wide) + dot(wu_t[...], nb[...])).astype(BF16)
+        final = (dot(we_t[...], wide) + dot(wu_t[...], nb[g % 2])).astype(BF16)
         values = dot(wd_t[...], final) + wide.astype(F32)
+        chunk, place = divmod(PARTS * g, members)
         for q in range(PARTS):
-            fs[pl.ds(pl.multiple_of((place * PARTS + q) * CHANNELS, CHANNELS), CHANNELS), :] = (
-                values[:, NODES * q : NODES * (q + 1)]
-            )
-
-    members = MEMBERS // MEMBER_CHUNKS
-    x_copies = []
-    for chunk in range(MEMBER_CHUNKS):
-        steps = groups // MEMBER_CHUNKS
-
-        def step(place, carry):
-            forecast(chunk * steps + place, place)
-            return carry
-
-        lax.fori_loop(0, steps, step, 0)
+            top = (place + q) * CHANNELS
+            fs[chunk % 2, top : top + CHANNELS, :] = values[:, NODES * q : NODES * (q + 1)]
+        if place + PARTS < members:
+            return
         packed = jnp.concatenate(
             [
                 jnp.concatenate(
                     [
-                        fs[pl.ds(PARTS * cg + c, members, stride=CHANNELS), :]
+                        fs[chunk % 2, pl.ds(PARTS * cg + c, members, stride=CHANNELS), :]
                         for c in range(PARTS)
                     ],
                     axis=1,
-                ).astype(BF16)
+                )
                 for cg in range(CHANNELS // PARTS)
             ],
             axis=0,
-        )
+        ).astype(BF16)
         turned = dot(packed, perm[...]).astype(BF16)
         for target in range(PARTS):
             sb[target, chunk] = turned[:, NODES * target : NODES * (target + 1)]
@@ -402,6 +422,14 @@
             copy.start()
             x_copies.append(copy)
         xr[row, chunk] = sb[row, chunk]
+
+    for g in range(groups + 2):
+        if g < groups:
+            gather(g)
+        if 1 <= g <= groups:
+            message(g - 1)
+        if g >= 2:
+            update(g - 2)
 
     for copy in sum_copies + far_copies:
         copy.wait_recv()
@@ -437,7 +465,16 @@
         - jnp.sum(root, axis=1, keepdims=True)
         - jnp.sum(mean_weights, axis=1, keepdims=True)
     ) * (1.0 / ENSEMBLE)
-    mix_high, mix_low = split(root + mean_weights + rest)
+    lane = iota((ENSEMBLE, 2 * ENSEMBLE), 1)
+    source = iota((ENSEMBLE, 2 * ENSEMBLE), 0)
+    same = ((lane >> 4) == (source >> 3)) & ((lane & 7) == (source & 7))
+    spread = [
+        jnp.where(same & (((lane >> 3) & 1) == half), 1.0, 0.0).astype(BF16) for half in range(2)
+    ]
+    mix_high, mix_low = [
+        jnp.concatenate([dot(part, s) for s in spread], axis=0).astype(BF16)
+        for part in split(root + mean_weights + rest)
+    ]
 
     for copy in x_copies:
         copy.wait_recv()
@@ -449,21 +486,22 @@
             [
                 jnp.concatenate(
                     [
-                        xr[source, chunk, members * cg : members * (cg + 1), :]
+                        xr[source, chunk, 16 * pair : 16 * (pair + 1), :]
                         for source in range(PARTS)
                         for chunk in range(MEMBER_CHUNKS)
                     ],
                     axis=0,
                 )
-                for cg in range(ch * per_chunk, (ch + 1) * per_chunk)
+                for pair in range(ch * per_chunk // 2, (ch + 1) * per_chunk // 2)
             ],
             axis=1,
         )
         mixed = (dot(mix_high, states) + dot(mix_low, states)).astype(BF16)
         for target in range(PARTS):
             for cg in range(per_chunk):
+                top = ENSEMBLE * (cg % 2) + owned * target
                 zs[target, ch, owned * cg : owned * (cg + 1), :] = mixed[
-                    owned * target : owned * (target + 1), NODES * cg : NODES * (cg + 1)
+                    top : top + owned, NODES * (cg // 2) : NODES * (cg // 2 + 1)
                 ]
         sent = []
         for d in range(1, PARTS):
@@ -504,19 +542,32 @@
 
 
 def body(*arrays):
+    arrays = list(arrays)
+    for i in (6, 7):
+        arrays[i] = arrays[i].T
     vmem = pl.BlockSpec(memory_space=pltpu.VMEM)
     dma = pltpu.SemaphoreType.DMA
     return pl.pallas_call(
         functools.partial(kernel, lax.axis_size("member"), lax.axis_size("space")),
         out_shape=jax.ShapeDtypeStruct((MEMBERS, CHANNELS, NODES), BF16),
-        in_specs=[pl.BlockSpec(memory_space=pl.ANY)] + [vmem] * 11,
+        in_specs=[pl.BlockSpec(memory_space=pl.ANY)] * 12,
         out_specs=vmem,
         scratch_shapes=[
             pltpu.VMEM((MEMBERS, CHANNELS, NODES), BF16),
+            pltpu.VMEM((CHANNELS, HIDDEN), BF16),
+            pltpu.VMEM((1, HIDDEN, HIDDEN), BF16),
+            pltpu.VMEM((1, HIDDEN, HIDDEN), BF16),
+            pltpu.VMEM((1, HIDDEN, HIDDEN), BF16),
+            pltpu.VMEM((1, HIDDEN), BF16),
+            pltpu.VMEM((CHANNELS, HIDDEN), BF16),
+            pltpu.VMEM((SLOTS, NODES), jnp.int32),
+            pltpu.VMEM((2, HALO), jnp.int32),
+            pltpu.VMEM((1, ENSEMBLE, HIDDEN), BF16),
+            pltpu.VMEM((1, 2, HIDDEN), BF16),
+            pltpu.VMEM((1, 8), jnp.int32),
             pltpu.VMEM((HIDDEN, CHANNELS), BF16),
             pltpu.VMEM((2 * HIDDEN, HIDDEN), BF16),
             pltpu.VMEM((HIDDEN, HIDDEN), BF16),
-            pltpu.VMEM((CHANNELS, HIDDEN), BF16),
             pltpu.VMEM((HIDDEN, NODES), F32),
             pltpu.VMEM((2, HIDDEN, SLOTS * NODES), BF16),
             pltpu.VMEM((PARTS * NODES, PARTS * NODES), BF16),
@@ -528,12 +579,12 @@
             pltpu.VMEM((MEMBERS, HIDDEN, NODES), BF16),
             pltpu.VMEM((MEMBERS, HIDDEN, NODES), F32),
             pltpu.VMEM((MEMBERS // 2, HIDDEN, NODES), BF16),
-            pltpu.VMEM((2 * HIDDEN, SLOTS * NODES), F32),
-            pltpu.VMEM((HIDDEN, NODES), F32),
-            pltpu.VMEM((HIDDEN, PARTS * NODES), BF16),
-            pltpu.VMEM((MEMBERS // MEMBER_CHUNKS * CHANNELS, NODES), F32),
-            pltpu.VMEM((PARTS, MEMBER_CHUNKS, 256, NODES), BF16),
-            pltpu.VMEM((PARTS, MEMBER_CHUNKS, 256, NODES), BF16),
+            pltpu.VMEM((2, 2, 2 * HIDDEN, SLOTS * NODES), F32),
+            pltpu.VMEM((PARTS, HIDDEN, NODES), F32),
+            pltpu.VMEM((2, HIDDEN, PARTS * NODES), BF16),
+            pltpu.VMEM((2, MEMBERS // MEMBER_CHUNKS * CHANNELS, NODES), F32),
+            pltpu.VMEM((PARTS, MEMBER_CHUNKS, 512 // MEMBER_CHUNKS, NODES), BF16),
+            pltpu.VMEM((PARTS, MEMBER_CHUNKS, 512 // MEMBER_CHUNKS, NODES), BF16),
             pltpu.VMEM((PARTS, CHANNEL_CHUNKS, 512 // CHANNEL_CHUNKS, NODES), BF16),
             pltpu.VMEM((PARTS, CHANNEL_CHUNKS, 512 // CHANNEL_CHUNKS, NODES), BF16),
             pltpu.VMEM((MEMBERS * CHANNELS // CHANNEL_CHUNKS, NODES), F32),
@@ -543,7 +594,7 @@
             pltpu.VMEM((2, GRAM_ROWS, ENSEMBLE), BF16),
             pltpu.VMEM((2, GRAM_ROWS, ENSEMBLE), BF16),
             pltpu.VMEM((2, GRAM_ROWS, ENSEMBLE), BF16),
-            dma,
+            dma((12,)),
             dma((2,)),
             dma((2,)),
             dma((2,)),

time: 68.5 us -> 61.8 us (0.902)
  Pallas kernels: 64.1 us -> 59.7 us
  local copies, waits for them, and re-layouts: 4.12 us -> 1.87 us
    pallas_call x1, Pallas kernels: 64.1 us -> 59.7 us  [body(): pl.pallas_call(functools.partial(kernel, lax.axis_size('member'), lax.axi...]
    unnamed x5 -> x1, local copies, waits for them, and re-layouts: 4.12 us -> 1.87 us
where the time goes in v2:
time: 61.8 us; the launch traced here: 61.6 us
  Pallas kernels  59.7 us (97%)
  local copies, waits for them, and re-layouts  1.87 us (3%)
    pallas_call x1, Pallas kernels, body(): pl.pallas_call(functools.partial(kernel, lax.axis_size('member'), lax.axi...  59.7 us
    unnamed x1, local copies, waits for them, and re-layouts  1.87 us

profile of v2, /device:TPU:8, one launch (start us, length us, event | category | flops | bytes accessed | tf_op | source)
XLA Modules:
  0.0 61.6 jit_solution(8486108783366343006)
XLA Ops:
  0.0 59.7 %cycle.1 = bf16[32,64,128]{2,1,0:T(8,128)(2,1)} custom-call(bf16[32,64,128]{2,1,0:T(8,128)(2,1)} %fields_hbm.1, bf16[64,256]{1,0:T(8,128)(2,1)} %we_hbm.1, bf16[1,256,256]{2,1,0:T(8,128)(2,1)} %ws_hbm.1, bf16[1,256,256]{2,1,0:T(8,128)(2,1)} %wr_hbm.1, bf16[1,256,256]{2,1,0:T(8,128)(2,1)} %wu_hbm.1, bf16[1,256]{1,0:T(2,128)(2,1)} %gain_hbm.1, ...), custom_call_target="tpu_custom_call" | custom-call | tf_op jit(solution)/shard_map/cycle/pallas_call | solution.py:550
  59.7 1.9 %copy.14 = bf16[32,64,128]{2,1,0:T(8,128)(2,1)} copy(bf16[32,64,128]{2,1,0:T(8,128)(2,1)} %cycle.1) | data formatting | bytes 1048576

commit v3 on v2

--- a/solution.py
+++ b/solution.py
@@ -25,7 +25,6 @@
 GRAM_ROWS = 144
 MEMBER_CHUNKS = 4
 CHANNEL_CHUNKS = 4
-HALO_STEP = 8
 OWN_STEP = 16
 
 
@@ -84,10 +83,8 @@
     gain_col,
     pick,
     perm,
-    perm_halo,
-    lists,
+    chooser,
     nears,
-    halo_send,
     halo_recv,
     se,
     rv,
@@ -108,8 +105,6 @@
     sum_recv,
     gram_far,
     load_sem,
-    list_send_sem,
-    list_recv_sem,
     near_send_sem,
     near_recv_sem,
     halo_send_sem,
@@ -162,15 +157,30 @@
         load.start()
 
     eye_hidden = eye(HIDDEN, BF16)
-    r1 = iota((HIDDEN, HIDDEN), 0)
-    goal = ((r1 >> 5) & 3) * (2 * HALO) + (r1 >> 7) * HALO + (r1 & 31)
-    perm_halo[...] = jnp.where(iota((HIDDEN, HIDDEN), 1) == goal, 1.0, 0.0).astype(BF16)
-    repeat = jnp.where(
-        iota((HALO, NODES), 0) == (iota((HALO, NODES), 1) & (HALO - 1)), 1.0, 0.0
-    ).astype(BF16)
-
     for load in loads[0:4]:
         load.wait()
+    repeat = jnp.where(
+        iota((HALO, HIDDEN), 0) == (iota((HALO, HIDDEN), 1) & (HALO - 1)), 1.0, 0.0
+    ).astype(BF16)
+    lane = iota((NODES, HIDDEN), 1)
+    after = ((lane >> 5) & 1) == 1
+    names = [
+        jnp.broadcast_to(
+            dot(
+                jnp.broadcast_to(halo_ref[i : i + 1, :].astype(F32), (8, HALO)).astype(BF16), repeat
+            )[0:1],
+            (NODES, HIDDEN),
+        )
+        for i in range(2)
+    ]
+    names = jnp.where(after, names[1], names[0]).astype(jnp.int32)
+    hit = names == iota((NODES, HIDDEN), 0)
+    for i in range(2):
+        for q in range(PARTS):
+            chosen = hit & (after == (i == 1)) & ((lane >> 6) == q)
+            top = NODES * (PARTS * i + q)
+            chooser[top : top + NODES, :] = jnp.where(chosen, 1.0, 0.0).astype(BF16)
+
     pert = pert_ref[0]
     variance = vals_ref[0, 0:1, :].astype(F32)
     innovation = vals_ref[0, 1:2, :].astype(F32)
@@ -199,18 +209,30 @@
     gram_own[ENSEMBLE:GRAM_ROWS, :] = forcing_rows(forcing)
     gram_send[...] = gram_own[...].astype(BF16)
 
+    for load in loads[4:]:
+        load.wait()
     pl.semaphore_wait(barrier, len(partners))
 
-    list_copies = []
-    for i, offset in enumerate((1, -1)):
-        list_copies.append(
-            remote(halo_ref, lists.at[i], list_send_sem.at[i], list_recv_sem.at[i], at_space(offset))
-        )
-        list_copies.append(
-            remote(near_ref, nears.at[i], near_send_sem.at[i], near_recv_sem.at[i], at_space(offset))
-        )
-    for copy in list_copies:
+    near_copies = [
+        remote(near_ref, nears.at[i], near_send_sem.at[i], near_recv_sem.at[i], at_space(offset))
+        for i, offset in enumerate((1, -1))
+    ]
+    for copy in near_copies:
         copy.start()
+    members = MEMBERS // MEMBER_CHUNKS
+    halo_copies = []
+    for chunk in range(MEMBER_CHUNKS):
+        part = pl.ds(members * chunk, members)
+        for i, offset in enumerate((1, -1)):
+            copy = remote(
+                fv.at[part],
+                halo_recv.at[i, part],
+                halo_send_sem.at[chunk, i],
+                halo_recv_sem.at[chunk, i],
+                at_space(offset),
+            )
+            copy.start()
+            halo_copies.append(copy)
     member_copies = [
         remote(gram_send, gram_member.at[i], gm_send_sem.at[i], gm_recv_sem.at[i], at_member(offset))
         for i, offset in enumerate((1, -1))
@@ -219,57 +241,14 @@
         remote(gram_send, gram_far.at[i], far_send_sem.at[i], far_recv_sem.at[i], at_space(offset))
         for i, offset in enumerate((2, -2))
     ]
-    for copy in member_copies:
+    for copy in member_copies + far_copies:
         copy.start()
 
-    for load in loads[4:]:
-        load.wait()
     we_t[...] = dot_nt(eye_hidden, we_ref[...]).astype(BF16)
     wsr_t[0:HIDDEN, :] = dot_nt(eye_hidden, ws_ref[0]).astype(BF16)
     wsr_t[HIDDEN:, :] = (dot_nt(eye_hidden, wr_ref[0]) * 0.5).astype(BF16)
 
-    for i in range(2):
-        list_copies[2 * i].wait_recv()
-
-    node = iota((NODES, HALO), 0)
-    block = iota((NODES, NODES), 1) >> 5
-    wanted = []
-    for names in (lists[1, 0:1, :], lists[0, 1:2, :]):
-        one_hot = jnp.where(node == jnp.broadcast_to(names, (NODES, HALO)), 1.0, 0.0).astype(BF16)
-        wanted.append(dot(one_hot, repeat))
-    chooser = jnp.concatenate(
-        [
-            jnp.concatenate([jnp.where(block == q, w, 0.0) for w in wanted], axis=1)
-            for q in range(PARTS)
-        ],
-        axis=0,
-    ).astype(BF16)
     groups = MEMBERS // PARTS
-    quads = jnp.concatenate(
-        [
-            jnp.concatenate([fv[PARTS * g + q] for g in range(groups)], axis=0)
-            for q in range(PARTS)
-        ],
-        axis=1,
-    )
-    chosen = dot(quads, chooser).astype(BF16)
-    halo_send[0] = chosen[:, 0:NODES]
-    halo_send[1] = chosen[:, NODES:]
-    halo_copies = [
-        remote(
-            halo_send.at[i],
-            halo_recv.at[i],
-            halo_send_sem.at[i],
-            halo_recv_sem.at[i],
-            at_space(offset),
-        )
-        for i, offset in enumerate((1, -1))
-    ]
-    for copy in halo_copies:
-        copy.start()
-    for copy in far_copies:
-        copy.start()
-
     for m in range(0, MEMBERS, OWN_STEP):
         wide = jnp.concatenate([fv[m + t] for t in range(OWN_STEP)], axis=1)
         rounded = dot(we_t[...], wide).astype(BF16)
@@ -292,6 +271,33 @@
     goal = ((r0 >> 5) & 3) * NODES + (r0 >> 7) * HALO + (r0 & 31)
     perm[...] = jnp.where(iota((wide_lanes, wide_lanes), 1) == goal, 1.0, 0.0).astype(BF16)
 
+    def halo(chunk):
+        for copy in halo_copies[2 * chunk : 2 * chunk + 2]:
+            copy.wait_recv()
+        first = members * chunk
+        both = jnp.concatenate(
+            [
+                jnp.concatenate(
+                    [
+                        halo_recv[i, first + PARTS * t + q]
+                        for i in range(2)
+                        for q in range(PARTS)
+                    ],
+                    axis=1,
+                )
+                for t in range(members // PARTS)
+            ],
+            axis=0,
+        )
+        ordered = dot(both, chooser[...]).astype(BF16)
+        wide = jnp.concatenate(
+            [ordered[CHANNELS * t : CHANNELS * (t + 1)] for t in range(members // PARTS)], axis=1
+        )
+        rounded = dot(we_t[...], wide).astype(BF16)
+        values = dot(wsr_t[0:HIDDEN, :], rounded).astype(BF16)
+        for t in range(members // 2):
+            sh[first // 2 + t] = values[:, NODES * t : NODES * (t + 1)]
+
     def region(p, s):
         r = lax.rem(row + p + member_count, member_count)
         c = lax.rem(column + s + space_count, space_count)
@@ -303,43 +309,28 @@
         )
         return held * (1.0 / (1.0 + (p * p + s * s) / 2.0))
 
-    for copy in member_copies:
-        copy.wait_recv()
-    for i in range(2):
-        list_copies[2 * i + 1].wait_recv()
-    rows = [(-1, gram_member[0].astype(F32)), (0, gram_own[...]), (1, gram_member[1].astype(F32))]
-    for i, (offset, s) in enumerate(((1, -1), (-1, 1))):
-        names = nears[1 - i]
-        total = sum(weight(names, p, s, offset) * values for p, values in rows)
-        sum_send[i, 0:ENSEMBLE, :] = total[0:ENSEMBLE].astype(BF16)
-        sum_send[i, ENSEMBLE:, :] = forcing_rows(
-            jnp.sum(total[ENSEMBLE:], axis=0, keepdims=True)
-        ).astype(BF16)
-    sum_copies = [
-        remote(
-            sum_send.at[i], sum_recv.at[i], sum_send_sem.at[i], sum_recv_sem.at[i], at_space(offset)
-        )
-        for i, offset in enumerate((1, -1))
-    ]
-    for copy in sum_copies:
-        copy.start()
-
-    for copy in halo_copies:
-        copy.wait_recv()
-
-    both = jnp.concatenate([halo_recv[0], halo_recv[1]], axis=1)
-    ordered = dot(both, perm_halo[...]).astype(BF16)
-    for g in range(0, groups, HALO_STEP):
-        wide = jnp.concatenate(
-            [ordered[CHANNELS * t : CHANNELS * (t + 1)] for t in range(g, g + HALO_STEP)], axis=1
-        )
-        rounded = dot(we_t[...], wide).astype(BF16)
-        values = dot(wsr_t[0:HIDDEN, :], rounded).astype(BF16)
-        for t in range(2 * HALO_STEP):
-            sh[2 * g + t] = values[:, NODES * t : NODES * (t + 1)]
-
+    sum_copies = []
+
+    def send_sums():
+        for copy in member_copies:
+            copy.wait_recv()
+        for copy in near_copies:
+            copy.wait_recv()
+        rows = [(-1, gram_member[0].astype(F32)), (0, gram_own[...]), (1, gram_member[1].astype(F32))]
+        for i, (offset, s) in enumerate(((1, -1), (-1, 1))):
+            names = nears[1 - i]
+            total = sum(weight(names, p, s, offset) * values for p, values in rows)
+            sum_send[i, 0:ENSEMBLE, :] = total[0:ENSEMBLE].astype(BF16)
+            sum_send[i, ENSEMBLE:, :] = forcing_rows(
+                jnp.sum(total[ENSEMBLE:], axis=0, keepdims=True)
+            ).astype(BF16)
+        for i, offset in enumerate((1, -1)):
+            copy = remote(
+                sum_send.at[i], sum_recv.at[i], sum_send_sem.at[i], sum_recv_sem.at[i], at_space(offset)
+            )
+            copy.start()
+            sum_copies.append(copy)
     strip = 64
-    members = MEMBERS // MEMBER_CHUNKS
     x_copies = []
 
     def gather(g):
@@ -423,13 +414,20 @@
             x_copies.append(copy)
         xr[row, chunk] = sb[row, chunk]
 
-    for g in range(groups + 2):
-        if g < groups:
-            gather(g)
-        if 1 <= g <= groups:
-            message(g - 1)
-        if g >= 2:
-            update(g - 2)
+    for chunk in range(MEMBER_CHUNKS):
+        halo(chunk)
+        first = chunk * members // PARTS
+        last = first + members // PARTS
+        gather(first)
+        for g in range(first, last):
+            if g + 1 < last:
+                gather(g + 1)
+            message(g)
+            if g > first:
+                update(g - 1)
+        update(last - 1)
+        if chunk == 0:
+            send_sums()
 
     for copy in sum_copies + far_copies:
         copy.wait_recv()
@@ -534,7 +532,7 @@
                 BF16
             )
 
-    for copy in list_copies + member_copies + far_copies + halo_copies + sum_copies + x_copies:
+    for copy in near_copies + member_copies + far_copies + halo_copies + sum_copies + x_copies:
         copy.wait_send()
     for sent in z_copies:
         for copy in sent:
@@ -571,11 +569,9 @@
             pltpu.VMEM((HIDDEN, NODES), F32),
             pltpu.VMEM((2, HIDDEN, SLOTS * NODES), BF16),
             pltpu.VMEM((PARTS * NODES, PARTS * NODES), BF16),
-            pltpu.VMEM((HIDDEN, HIDDEN), BF16),
-            pltpu.VMEM((2, 2, HALO), jnp.int32),
+            pltpu.VMEM((2 * PARTS * NODES, HIDDEN), BF16),
             pltpu.VMEM((2, 1, 8), jnp.int32),
-            pltpu.VMEM((2, MEMBERS // PARTS * CHANNELS, NODES), BF16),
-            pltpu.VMEM((2, MEMBERS // PARTS * CHANNELS, NODES), BF16),
+            pltpu.VMEM((2, MEMBERS, CHANNELS, NODES), BF16),
             pltpu.VMEM((MEMBERS, HIDDEN, NODES), BF16),
             pltpu.VMEM((MEMBERS, HIDDEN, NODES), F32),
             pltpu.VMEM((MEMBERS // 2, HIDDEN, NODES), BF16),
@@ -597,10 +593,8 @@
             dma((12,)),
             dma((2,)),
             dma((2,)),
-            dma((2,)),
-            dma((2,)),
-            dma((2,)),
-            dma((2,)),
+            dma((MEMBER_CHUNKS, 2)),
+            dma((MEMBER_CHUNKS, 2)),
             dma((2,)),
             dma((2,)),
             dma((2,)),

time: 61.8 us -> 62.2 us (level)
  no operation moved by 1% of the time
where the time goes in v3:
time: 62.2 us; the launch traced here: 62 us
  Pallas kernels  60.1 us (97%)
  local copies, waits for them, and re-layouts  1.87 us (3%)
    pallas_call x1, Pallas kernels, body(): pl.pallas_call(functools.partial(kernel, lax.axis_size('member'), lax.axi...  60.1 us
    unnamed x1, local copies, waits for them, and re-layouts  1.87 us

profile of v3, /device:TPU:8, one launch (start us, length us, event | category | flops | bytes accessed | tf_op | source)
XLA Modules:
  0.0 62.0 jit_solution(7579709101202171561)
XLA Ops:
  0.0 60.1 %cycle.1 = bf16[32,64,128]{2,1,0:T(8,128)(2,1)} custom-call(bf16[32,64,128]{2,1,0:T(8,128)(2,1)} %fields_hbm.1, bf16[64,256]{1,0:T(8,128)(2,1)} %we_hbm.1, bf16[1,256,256]{2,1,0:T(8,128)(2,1)} %ws_hbm.1, bf16[1,256,256]{2,1,0:T(8,128)(2,1)} %wr_hbm.1, bf16[1,256,256]{2,1,0:T(8,128)(2,1)} %wu_hbm.1, bf16[1,256]{1,0:T(2,128)(2,1)} %gain_hbm.1, ...), custom_call_target="tpu_custom_call" | custom-call | tf_op jit(solution)/shard_map/cycle/pallas_call | solution.py:548
  60.1 1.9 %copy.14 = bf16[32,64,128]{2,1,0:T(8,128)(2,1)} copy(bf16[32,64,128]{2,1,0:T(8,128)(2,1)} %cycle.1) | data formatting | bytes 1048576

commit v4 on v3

--- a/solution.py
+++ b/solution.py
@@ -84,8 +84,11 @@
     pick,
     perm,
     chooser,
+    lists,
     nears,
     halo_recv,
+    side_send,
+    side_recv,
     se,
     rv,
     sh,
@@ -103,18 +106,22 @@
     gram_member,
     sum_send,
     sum_recv,
-    gram_far,
+    gram_side,
     load_sem,
+    list_send_sem,
+    list_recv_sem,
     near_send_sem,
     near_recv_sem,
     halo_send_sem,
     halo_recv_sem,
+    side_send_sem,
+    side_recv_sem,
     gm_send_sem,
     gm_recv_sem,
     sum_send_sem,
     sum_recv_sem,
-    far_send_sem,
-    far_recv_sem,
+    gs_send_sem,
+    gs_recv_sem,
     x_send_sem,
     x_recv_sem,
     z_send_sem,
@@ -140,8 +147,7 @@
         )
 
     barrier = pltpu.get_barrier_semaphore()
-    partners = [at_space(-1), at_space(1), at_space(-2), at_space(2)]
-    partners += [at_member(d) for d in range(1, PARTS)]
+    partners = [at_space(-1)] + [at_member(d) for d in range(1, PARTS)]
     for partner in partners:
         pl.semaphore_signal(barrier, inc=1, device_id=partner, device_id_type=MESH)
 
@@ -164,22 +170,19 @@
     ).astype(BF16)
     lane = iota((NODES, HIDDEN), 1)
     after = ((lane >> 5) & 1) == 1
-    names = [
-        jnp.broadcast_to(
-            dot(
-                jnp.broadcast_to(halo_ref[i : i + 1, :].astype(F32), (8, HALO)).astype(BF16), repeat
-            )[0:1],
-            (NODES, HIDDEN),
-        )
-        for i in range(2)
-    ]
-    names = jnp.where(after, names[1], names[0]).astype(jnp.int32)
-    hit = names == iota((NODES, HIDDEN), 0)
-    for i in range(2):
-        for q in range(PARTS):
-            chosen = hit & (after == (i == 1)) & ((lane >> 6) == q)
-            top = NODES * (PARTS * i + q)
-            chooser[top : top + NODES, :] = jnp.where(chosen, 1.0, 0.0).astype(BF16)
+
+
+    def spread_names(values):
+        values = jnp.broadcast_to(values.astype(F32), (8, HALO)).astype(BF16)
+        return jnp.broadcast_to(dot(values, repeat)[0:1], (NODES, HIDDEN)).astype(jnp.int32)
+
+    hit = spread_names(halo_ref[0:1, :]) == iota((NODES, HIDDEN), 0)
+    for q in range(PARTS):
+        chosen = hit & jnp.logical_not(after) & ((lane >> 6) == q)
+        chooser[NODES * q : NODES * (q + 1), :] = jnp.where(chosen, 1.0, 0.0).astype(BF16)
+    kept = iota((NODES, HIDDEN), 0)
+    kept = (kept >> 5) * (2 * HALO) + HALO + (kept & (HALO - 1))
+    chooser[PARTS * NODES :, :] = jnp.where(lane == kept, 1.0, 0.0).astype(BF16)
 
     pert = pert_ref[0]
     variance = vals_ref[0, 0:1, :].astype(F32)
@@ -213,35 +216,37 @@
         load.wait()
     pl.semaphore_wait(barrier, len(partners))
 
+    list_copy = remote(halo_ref, lists, list_send_sem, list_recv_sem, at_space(1))
     near_copies = [
         remote(near_ref, nears.at[i], near_send_sem.at[i], near_recv_sem.at[i], at_space(offset))
         for i, offset in enumerate((1, -1))
     ]
-    for copy in near_copies:
-        copy.start()
+    side_copies = [
+        remote(gram_send, gram_side.at[i], gs_send_sem.at[i], gs_recv_sem.at[i], at_space(offset))
+        for i, offset in enumerate((1, -1))
+    ]
+    member_copies = [
+        remote(gram_send, gram_member.at[i], gm_send_sem.at[i], gm_recv_sem.at[i], at_member(offset))
+        for i, offset in enumerate((1, -1))
+    ]
+    list_copy.start()
+    near_copies[0].start()
     members = MEMBERS // MEMBER_CHUNKS
     halo_copies = []
     for chunk in range(MEMBER_CHUNKS):
         part = pl.ds(members * chunk, members)
-        for i, offset in enumerate((1, -1)):
-            copy = remote(
-                fv.at[part],
-                halo_recv.at[i, part],
-                halo_send_sem.at[chunk, i],
-                halo_recv_sem.at[chunk, i],
-                at_space(offset),
-            )
-            copy.start()
-            halo_copies.append(copy)
-    member_copies = [
-        remote(gram_send, gram_member.at[i], gm_send_sem.at[i], gm_recv_sem.at[i], at_member(offset))
-        for i, offset in enumerate((1, -1))
-    ]
-    far_copies = [
-        remote(gram_send, gram_far.at[i], far_send_sem.at[i], far_recv_sem.at[i], at_space(offset))
-        for i, offset in enumerate((2, -2))
-    ]
-    for copy in member_copies + far_copies:
+        copy = remote(
+            fv.at[part],
+            halo_recv.at[part],
+            halo_send_sem.at[chunk],
+            halo_recv_sem.at[chunk],
+            at_space(1),
+        )
+        copy.start()
+        halo_copies.append(copy)
+        if chunk == 0:
+            side_copies[0].start()
+    for copy in member_copies:
         copy.start()
 
     we_t[...] = dot_nt(eye_hidden, we_ref[...]).astype(BF16)
@@ -271,18 +276,46 @@
     goal = ((r0 >> 5) & 3) * NODES + (r0 >> 7) * HALO + (r0 & 31)
     perm[...] = jnp.where(iota((wide_lanes, wide_lanes), 1) == goal, 1.0, 0.0).astype(BF16)
 
+    list_copy.wait_recv()
+    near_copies[0].wait_recv()
+    near_copies[1].start()
+    hit = spread_names(lists[1:2, :])[:, 0:NODES] == iota((NODES, NODES), 0)
+    block = iota((NODES, NODES), 1) >> 5
+    wanted = jnp.concatenate(
+        [jnp.where(hit & (block == q), 1.0, 0.0).astype(BF16) for q in range(PARTS)], axis=0
+    )
+    quads = jnp.concatenate(
+        [
+            jnp.concatenate([fv[PARTS * g + q] for g in range(groups)], axis=0)
+            for q in range(PARTS)
+        ],
+        axis=1,
+    )
+    side_send[...] = dot(quads, wanted).astype(BF16)
+    side_rows = members // PARTS * CHANNELS
+    select_copies = []
+    for chunk in range(MEMBER_CHUNKS):
+        part = pl.ds(side_rows * chunk, side_rows)
+        copy = remote(
+            side_send.at[part],
+            side_recv.at[part],
+            side_send_sem.at[chunk],
+            side_recv_sem.at[chunk],
+            at_space(-1),
+        )
+        copy.start()
+        select_copies.append(copy)
+    side_copies[1].start()
+
     def halo(chunk):
-        for copy in halo_copies[2 * chunk : 2 * chunk + 2]:
-            copy.wait_recv()
+        halo_copies[chunk].wait_recv()
+        select_copies[chunk].wait_recv()
         first = members * chunk
         both = jnp.concatenate(
             [
                 jnp.concatenate(
-                    [
-                        halo_recv[i, first + PARTS * t + q]
-                        for i in range(2)
-                        for q in range(PARTS)
-                    ],
+                    [halo_recv[first + PARTS * t + q] for q in range(PARTS)]
+                    + [side_recv[CHANNELS * (first // PARTS + t) : CHANNELS * (first // PARTS + t + 1), :]],
                     axis=1,
                 )
                 for t in range(members // PARTS)
@@ -311,25 +344,33 @@
 
     sum_copies = []
 
-    def send_sums():
-        for copy in member_copies:
-            copy.wait_recv()
-        for copy in near_copies:
-            copy.wait_recv()
-        rows = [(-1, gram_member[0].astype(F32)), (0, gram_own[...]), (1, gram_member[1].astype(F32))]
-        for i, (offset, s) in enumerate(((1, -1), (-1, 1))):
-            names = nears[1 - i]
-            total = sum(weight(names, p, s, offset) * values for p, values in rows)
-            sum_send[i, 0:ENSEMBLE, :] = total[0:ENSEMBLE].astype(BF16)
-            sum_send[i, ENSEMBLE:, :] = forcing_rows(
-                jnp.sum(total[ENSEMBLE:], axis=0, keepdims=True)
-            ).astype(BF16)
-        for i, offset in enumerate((1, -1)):
-            copy = remote(
-                sum_send.at[i], sum_recv.at[i], sum_send_sem.at[i], sum_recv_sem.at[i], at_space(offset)
-            )
-            copy.start()
-            sum_copies.append(copy)
+    def send_sum(i):
+        offset, s = ((1, -1), (-1, 1))[i]
+        if i == 0:
+            near_copies[1].wait_recv()
+        side_copies[i].wait_recv()
+        names = nears[1 - i]
+        rows = [
+            (-1, gram_member[0].astype(F32)),
+            (0, gram_own[...]),
+            (1, gram_member[1].astype(F32)),
+        ]
+        total = sum(weight(names, p, s, offset) * values for p, values in rows)
+        total = total + weight(names, 0, 2 * s, offset) * gram_side[i].astype(F32)
+        sum_send[i, 0:ENSEMBLE, :] = total[0:ENSEMBLE].astype(BF16)
+        sum_send[i, ENSEMBLE:, :] = forcing_rows(
+            jnp.sum(total[ENSEMBLE:], axis=0, keepdims=True)
+        ).astype(BF16)
+        copy = remote(
+            sum_send.at[i], sum_recv.at[i], sum_send_sem.at[i], sum_recv_sem.at[i], at_space(offset)
+        )
+        copy.start()
+        sum_copies.append(copy)
+
+    for copy in member_copies:
+        copy.wait_recv()
+    send_sum(0)
+
     strip = 64
     x_copies = []
 
@@ -427,17 +468,15 @@
                 update(g - 1)
         update(last - 1)
         if chunk == 0:
-            send_sums()
-
-    for copy in sum_copies + far_copies:
+            send_sum(1)
+
+    for copy in sum_copies:
         copy.wait_recv()
     names = near_ref[...]
     total = gram_own[...] + sum_recv[0].astype(F32) + sum_recv[1].astype(F32)
     for values, p, s in (
         (gram_member[0], -1, 0),
         (gram_member[1], 1, 0),
-        (gram_far[0], 0, -2),
-        (gram_far[1], 0, 2),
     ):
         total = total + weight(names, p, s, 0) * values.astype(F32)
     forcing = jnp.sum(total[ENSEMBLE:], axis=0, keepdims=True)
@@ -532,7 +571,8 @@
                 BF16
             )
 
-    for copy in near_copies + member_copies + far_copies + halo_copies + sum_copies + x_copies:
+    copies = [list_copy] + near_copies + side_copies + member_copies + halo_copies + select_copies
+    for copy in copies + sum_copies + x_copies:
         copy.wait_send()
     for sent in z_copies:
         for copy in sent:
@@ -569,9 +609,12 @@
             pltpu.VMEM((HIDDEN, NODES), F32),
             pltpu.VMEM((2, HIDDEN, SLOTS * NODES), BF16),
             pltpu.VMEM((PARTS * NODES, PARTS * NODES), BF16),
-            pltpu.VMEM((2 * PARTS * NODES, HIDDEN), BF16),
+            pltpu.VMEM(((PARTS + 1) * NODES, HIDDEN), BF16),
+            pltpu.VMEM((2, HALO), jnp.int32),
             pltpu.VMEM((2, 1, 8), jnp.int32),
-            pltpu.VMEM((2, MEMBERS, CHANNELS, NODES), BF16),
+            pltpu.VMEM((MEMBERS, CHANNELS, NODES), BF16),
+            pltpu.VMEM((MEMBERS // PARTS * CHANNELS, NODES), BF16),
+            pltpu.VMEM((MEMBERS // PARTS * CHANNELS, NODES), BF16),
             pltpu.VMEM((MEMBERS, HIDDEN, NODES), BF16),
             pltpu.VMEM((MEMBERS, HIDDEN, NODES), F32),
             pltpu.VMEM((MEMBERS // 2, HIDDEN, NODES), BF16),
@@ -591,10 +634,14 @@
             pltpu.VMEM((2, GRAM_ROWS, ENSEMBLE), BF16),
             pltpu.VMEM((2, GRAM_ROWS, ENSEMBLE), BF16),
             dma((12,)),
-            dma((2,)),
-            dma((2,)),
-            dma((MEMBER_CHUNKS, 2)),
-            dma((MEMBER_CHUNKS, 2)),
+            dma,
+            dma,
+            dma((2,)),
+            dma((2,)),
+            dma((MEMBER_CHUNKS,)),
+            dma((MEMBER_CHUNKS,)),
+            dma((MEMBER_CHUNKS,)),
+            dma((MEMBER_CHUNKS,)),
             dma((2,)),
             dma((2,)),
             dma((2,)),

time: 62.2 us -> 53.6 us (0.86)
  Pallas kernels: 60.1 us -> 51.6 us
    pallas_call x1, Pallas kernels: 60.1 us -> 51.6 us  [body(): pl.pallas_call(functools.partial(kernel, lax.axis_size('member'), lax.axi...]
where the time goes in v4:
time: 53.6 us; the launch traced here: 53.4 us
  Pallas kernels  51.6 us (96%)
  local copies, waits for them, and re-layouts  1.87 us (3%)
    pallas_call x1, Pallas kernels, body(): pl.pallas_call(functools.partial(kernel, lax.axis_size('member'), lax.axi...  51.6 us
    unnamed x1, local copies, waits for them, and re-layouts  1.87 us

profile of v4, /device:TPU:8, one launch (start us, length us, event | category | flops | bytes accessed | tf_op | source)
XLA Modules:
  0.0 53.4 jit_solution(17223936564949757671)
XLA Ops:
  0.0 51.6 %cycle.1 = bf16[32,64,128]{2,1,0:T(8,128)(2,1)} custom-call(bf16[32,64,128]{2,1,0:T(8,128)(2,1)} %fields_hbm.1, bf16[64,256]{1,0:T(8,128)(2,1)} %we_hbm.1, bf16[1,256,256]{2,1,0:T(8,128)(2,1)} %ws_hbm.1, bf16[1,256,256]{2,1,0:T(8,128)(2,1)} %wr_hbm.1, bf16[1,256,256]{2,1,0:T(8,128)(2,1)} %wu_hbm.1, bf16[1,256]{1,0:T(2,128)(2,1)} %gain_hbm.1, ...), custom_call_target="tpu_custom_call" | custom-call | tf_op jit(solution)/shard_map/cycle/pallas_call | solution.py:588
  51.6 1.9 %copy.14 = bf16[32,64,128]{2,1,0:T(8,128)(2,1)} copy(bf16[32,64,128]{2,1,0:T(8,128)(2,1)} %cycle.1) | data formatting | bytes 1048576

commit v5 on v4

--- a/solution.py
+++ b/solution.py
@@ -162,28 +162,43 @@
     for load in loads:
         load.start()
 
-    eye_hidden = eye(HIDDEN, BF16)
-    for load in loads[0:4]:
+    for load in (loads[0], loads[1], loads[7]):
         load.wait()
-    repeat = jnp.where(
-        iota((HALO, HIDDEN), 0) == (iota((HALO, HIDDEN), 1) & (HALO - 1)), 1.0, 0.0
-    ).astype(BF16)
-    lane = iota((NODES, HIDDEN), 1)
-    after = ((lane >> 5) & 1) == 1
-
-
-    def spread_names(values):
-        values = jnp.broadcast_to(values.astype(F32), (8, HALO)).astype(BF16)
-        return jnp.broadcast_to(dot(values, repeat)[0:1], (NODES, HIDDEN)).astype(jnp.int32)
-
-    hit = spread_names(halo_ref[0:1, :]) == iota((NODES, HIDDEN), 0)
-    for q in range(PARTS):
-        chosen = hit & jnp.logical_not(after) & ((lane >> 6) == q)
-        chooser[NODES * q : NODES * (q + 1), :] = jnp.where(chosen, 1.0, 0.0).astype(BF16)
-    kept = iota((NODES, HIDDEN), 0)
-    kept = (kept >> 5) * (2 * HALO) + HALO + (kept & (HALO - 1))
-    chooser[PARTS * NODES :, :] = jnp.where(lane == kept, 1.0, 0.0).astype(BF16)
-
+    pl.semaphore_wait(barrier, len(partners))
+
+    list_copy = remote(halo_ref, lists, list_send_sem, list_recv_sem, at_space(1))
+    near_copies = [
+        remote(near_ref, nears.at[i], near_send_sem.at[i], near_recv_sem.at[i], at_space(offset))
+        for i, offset in enumerate((1, -1))
+    ]
+    side_copies = [
+        remote(gram_send, gram_side.at[i], gs_send_sem.at[i], gs_recv_sem.at[i], at_space(offset))
+        for i, offset in enumerate((1, -1))
+    ]
+    member_copies = [
+        remote(gram_send, gram_member.at[i], gm_send_sem.at[i], gm_recv_sem.at[i], at_member(offset))
+        for i, offset in enumerate((1, -1))
+    ]
+    members = MEMBERS // MEMBER_CHUNKS
+    halo_copies = []
+    for chunk in range(MEMBER_CHUNKS):
+        part = pl.ds(members * chunk, members)
+        halo_copies.append(
+            remote(
+                fv.at[part],
+                halo_recv.at[part],
+                halo_send_sem.at[chunk],
+                halo_recv_sem.at[chunk],
+                at_space(1),
+            )
+        )
+    list_copy.start()
+    near_copies[0].start()
+    for copy in halo_copies[0:2]:
+        copy.start()
+
+    for load in loads[2:4]:
+        load.wait()
     pert = pert_ref[0]
     variance = vals_ref[0, 0:1, :].astype(F32)
     innovation = vals_ref[0, 1:2, :].astype(F32)
@@ -212,43 +227,32 @@
     gram_own[ENSEMBLE:GRAM_ROWS, :] = forcing_rows(forcing)
     gram_send[...] = gram_own[...].astype(BF16)
 
-    for load in loads[4:]:
+    side_copies[0].start()
+    for copy in member_copies + halo_copies[2:]:
+        copy.start()
+
+    eye_hidden = eye(HIDDEN, BF16)
+    repeat = jnp.where(
+        iota((HALO, HIDDEN), 0) == (iota((HALO, HIDDEN), 1) & (HALO - 1)), 1.0, 0.0
+    ).astype(BF16)
+    lane = iota((NODES, HIDDEN), 1)
+    after = ((lane >> 5) & 1) == 1
+
+
+    def spread_names(values):
+        values = jnp.broadcast_to(values.astype(F32), (8, HALO)).astype(BF16)
+        return jnp.broadcast_to(dot(values, repeat)[0:1], (NODES, HIDDEN)).astype(jnp.int32)
+
+    hit = spread_names(halo_ref[0:1, :]) == iota((NODES, HIDDEN), 0)
+    for q in range(PARTS):
+        chosen = hit & jnp.logical_not(after) & ((lane >> 6) == q)
+        chooser[NODES * q : NODES * (q + 1), :] = jnp.where(chosen, 1.0, 0.0).astype(BF16)
+    kept = iota((NODES, HIDDEN), 0)
+    kept = (kept >> 5) * (2 * HALO) + HALO + (kept & (HALO - 1))
+    chooser[PARTS * NODES :, :] = jnp.where(lane == kept, 1.0, 0.0).astype(BF16)
+
+    for load in loads[4:7] + loads[8:]:
         load.wait()
-    pl.semaphore_wait(barrier, len(partners))
-
-    list_copy = remote(halo_ref, lists, list_send_sem, list_recv_sem, at_space(1))
-    near_copies = [
-        remote(near_ref, nears.at[i], near_send_sem.at[i], near_recv_sem.at[i], at_space(offset))
-        for i, offset in enumerate((1, -1))
-    ]
-    side_copies = [
-        remote(gram_send, gram_side.at[i], gs_send_sem.at[i], gs_recv_sem.at[i], at_space(offset))
-        for i, offset in enumerate((1, -1))
-    ]
-    member_copies = [
-        remote(gram_send, gram_member.at[i], gm_send_sem.at[i], gm_recv_sem.at[i], at_member(offset))
-        for i, offset in enumerate((1, -1))
-    ]
-    list_copy.start()
-    near_copies[0].start()
-    members = MEMBERS // MEMBER_CHUNKS
-    halo_copies = []
-    for chunk in range(MEMBER_CHUNKS):
-        part = pl.ds(members * chunk, members)
-        copy = remote(
-            fv.at[part],
-            halo_recv.at[part],
-            halo_send_sem.at[chunk],
-            halo_recv_sem.at[chunk],
-            at_space(1),
-        )
-        copy.start()
-        halo_copies.append(copy)
-        if chunk == 0:
-            side_copies[0].start()
-    for copy in member_copies:
-        copy.start()
-
     we_t[...] = dot_nt(eye_hidden, we_ref[...]).astype(BF16)
     wsr_t[0:HIDDEN, :] = dot_nt(eye_hidden, ws_ref[0]).astype(BF16)
     wsr_t[HIDDEN:, :] = (dot_nt(eye_hidden, wr_ref[0]) * 0.5).astype(BF16)
@@ -585,9 +589,9 @@
         arrays[i] = arrays[i].T
     vmem = pl.BlockSpec(memory_space=pltpu.VMEM)
     dma = pltpu.SemaphoreType.DMA
-    return pl.pallas_call(
+    result = pl.pallas_call(
         functools.partial(kernel, lax.axis_size("member"), lax.axis_size("space")),
-        out_shape=jax.ShapeDtypeStruct((MEMBERS, CHANNELS, NODES), BF16),
+        out_shape=pltpu.VMEM((MEMBERS, CHANNELS, NODES), BF16),
         in_specs=[pl.BlockSpec(memory_space=pl.ANY)] * 12,
         out_specs=vmem,
         scratch_shapes=[
@@ -657,6 +661,20 @@
         name="cycle",
     )(*arrays)
 
+    def hand_on(source, target, sem):
+        copy = pltpu.make_async_copy(source, target, sem)
+        copy.start()
+        copy.wait()
+
+    return pl.pallas_call(
+        hand_on,
+        out_shape=jax.ShapeDtypeStruct((MEMBERS, CHANNELS, NODES), BF16),
+        in_specs=[vmem],
+        out_specs=pl.BlockSpec(memory_space=pl.ANY),
+        scratch_shapes=[dma],
+        name="hand_on",
+    )(pltpu.with_memory_space_constraint(result, pltpu.VMEM))
+
 
 def solution(mesh):
     placed = (

time: 53.6 us -> 52.3 us (0.976)
  local copies, waits for them, and re-layouts: 1.87 us -> 0 us
    unnamed x1 -> x0, local copies, waits for them, and re-layouts: 1.87 us -> none
    pallas_call x0 -> x1, Pallas kernels: none -> 0.8 us  [body(): pl.pallas_call(hand_on, out_shape=jax.ShapeDtypeStruct((MEMBERS, CHANNELS...]
where the time goes in v5:
time: 52.3 us; the launch traced here: 52.1 us
  Pallas kernels  52.1 us (100%)
    pallas_call x1, Pallas kernels, body(): pl.pallas_call(functools.partial(kernel, lax.axis_size('member'), lax.axi...  51.3 us

profile of v5, /device:TPU:8, one launch (start us, length us, event | category | flops | bytes accessed | tf_op | source)
XLA Modules:
  0.0 52.1 jit_solution(13797655095339842417)
XLA Ops:
  0.0 51.3 %cycle.1.source = bf16[32,64,128]{2,1,0:T(8,128)(2,1)S(1)} custom-call(bf16[32,64,128]{2,1,0:T(8,128)(2,1)} %fields_hbm.1, bf16[64,256]{1,0:T(8,128)(2,1)} %we_hbm.1, bf16[1,256,256]{2,1,0:T(8,128)(2,1)} %ws_hbm.1, bf16[1,256,256]{2,1,0:T(8,128)(2,1)} %wr_hbm.1, bf16[1,256,256]{2,1,0:T(8,128)(2,1)} %wu_hbm.1, bf16[1,256]{1,0:T(2,128)(2,1)} %gain_hbm.1, ...), custom_call_target="tpu_custom_call" | custom-call | tf_op jit(solution)/shard_map/cycle/pallas_call | solution.py:592
  51.3 0.8 %hand_on.1 = bf16[32,64,128]{2,1,0:T(8,128)(2,1)} custom-call(bf16[32,64,128]{2,1,0:T(8,128)(2,1)S(1)} %cycle.1.source), custom_call_target="tpu_custom_call" | custom-call | tf_op jit(solution)/shard_map/hand_on/pallas_call | solution.py:669

commit v6 on v5

--- a/solution.py
+++ b/solution.py
@@ -162,6 +162,36 @@
     for load in loads:
         load.start()
 
+    for load in loads[2:4]:
+        load.wait()
+    pert = pert_ref[0]
+    variance = vals_ref[0, 0:1, :].astype(F32)
+    innovation = vals_ref[0, 1:2, :].astype(F32)
+    scaled_high, scaled_low = split(pert.astype(F32) * variance)
+    gram = dot_nt(scaled_high, pert) + dot_nt(scaled_low, pert)
+    force_high, force_low = split(variance * innovation)
+    sub = iota((16, HIDDEN), 0)
+    force_rows = jnp.where(
+        sub == 0,
+        jnp.broadcast_to(force_high.astype(F32), (16, HIDDEN)),
+        jnp.where(sub == 1, jnp.broadcast_to(force_low.astype(F32), (16, HIDDEN)), 0.0),
+    ).astype(BF16)
+    forcing = jnp.sum(dot_nt(force_rows, pert), axis=0, keepdims=True)
+    sub16 = iota((16, ENSEMBLE), 0)
+
+    def forcing_rows(values):
+        high = values.astype(BF16).astype(F32)
+        low = values - high
+        return jnp.where(
+            sub16 == 0,
+            jnp.broadcast_to(high, (16, ENSEMBLE)),
+            jnp.where(sub16 == 1, jnp.broadcast_to(low, (16, ENSEMBLE)), 0.0),
+        )
+
+    gram_own[0:ENSEMBLE, :] = gram
+    gram_own[ENSEMBLE:GRAM_ROWS, :] = forcing_rows(forcing)
+    gram_send[...] = gram_own[...].astype(BF16)
+
     for load in (loads[0], loads[1], loads[7]):
         load.wait()
     pl.semaphore_wait(barrier, len(partners))
@@ -194,41 +224,11 @@
         )
     list_copy.start()
     near_copies[0].start()
+    side_copies[0].start()
     for copy in halo_copies[0:2]:
         copy.start()
 
-    for load in loads[2:4]:
-        load.wait()
-    pert = pert_ref[0]
-    variance = vals_ref[0, 0:1, :].astype(F32)
-    innovation = vals_ref[0, 1:2, :].astype(F32)
-    scaled_high, scaled_low = split(pert.astype(F32) * variance)
-    gram = dot_nt(scaled_high, pert) + dot_nt(scaled_low, pert)
-    force_high, force_low = split(variance * innovation)
-    sub = iota((16, HIDDEN), 0)
-    force_rows = jnp.where(
-        sub == 0,
-        jnp.broadcast_to(force_high.astype(F32), (16, HIDDEN)),
-        jnp.where(sub == 1, jnp.broadcast_to(force_low.astype(F32), (16, HIDDEN)), 0.0),
-    ).astype(BF16)
-    forcing = jnp.sum(dot_nt(force_rows, pert), axis=0, keepdims=True)
-    sub16 = iota((16, ENSEMBLE), 0)
-
-    def forcing_rows(values):
-        high = values.astype(BF16).astype(F32)
-        low = values - high
-        return jnp.where(
-            sub16 == 0,
-            jnp.broadcast_to(high, (16, ENSEMBLE)),
-            jnp.where(sub16 == 1, jnp.broadcast_to(low, (16, ENSEMBLE)), 0.0),
-        )
-
-    gram_own[0:ENSEMBLE, :] = gram
-    gram_own[ENSEMBLE:GRAM_ROWS, :] = forcing_rows(forcing)
-    gram_send[...] = gram_own[...].astype(BF16)
-
-    side_copies[0].start()
-    for copy in member_copies + halo_copies[2:]:
+    for copy in member_copies:
         copy.start()
 
     eye_hidden = eye(HIDDEN, BF16)
@@ -253,6 +253,9 @@
 
     for load in loads[4:7] + loads[8:]:
         load.wait()
+    halo_copies[0].wait_send()
+    halo_copies[2].start()
+
     we_t[...] = dot_nt(eye_hidden, we_ref[...]).astype(BF16)
     wsr_t[0:HIDDEN, :] = dot_nt(eye_hidden, ws_ref[0]).astype(BF16)
     wsr_t[HIDDEN:, :] = (dot_nt(eye_hidden, wr_ref[0]) * 0.5).astype(BF16)
@@ -266,6 +269,8 @@
             se[m + t] = both[0:HIDDEN, NODES * t : NODES * (t + 1)].astype(BF16)
             rv[m + t] = both[HIDDEN:, NODES * t : NODES * (t + 1)]
 
+    halo_copies[1].wait_send()
+    halo_copies[3].start()
     wu_t[...] = dot_nt(eye_hidden, wu_ref[0]).astype(BF16)
     gain_col[...] = dot_nt(eye_hidden, jnp.broadcast_to(gain_ref[...], (NODES, HIDDEN)))
     tall = iota((HIDDEN, NODES), 0)
@@ -575,7 +580,7 @@
                 BF16
             )
 
-    copies = [list_copy] + near_copies + side_copies + member_copies + halo_copies + select_copies
+    copies = [list_copy] + near_copies + side_copies + member_copies + halo_copies[2:] + select_copies
     for copy in copies + sum_copies + x_copies:
         copy.wait_send()
     for sent in z_copies:

time: 52.3 us -> 49.7 us (0.950)
  Pallas kernels: 52.1 us -> 49.6 us
    pallas_call x1, Pallas kernels: 51.3 us -> 48.8 us  [body(): pl.pallas_call(functools.partial(kernel, lax.axis_size('member'), lax.axi...]
where the time goes in v6:
time: 49.7 us; the launch traced here: 49.6 us
  Pallas kernels  49.6 us (100%)
    pallas_call x1, Pallas kernels, body(): pl.pallas_call(functools.partial(kernel, lax.axis_size('member'), lax.axi...  48.8 us

profile of v6, /device:TPU:8, one launch (start us, length us, event | category | flops | bytes accessed | tf_op | source)
XLA Modules:
  0.0 49.6 jit_solution(16160564087015056285)
XLA Ops:
  0.0 48.8 %cycle.1.source = bf16[32,64,128]{2,1,0:T(8,128)(2,1)S(1)} custom-call(bf16[32,64,128]{2,1,0:T(8,128)(2,1)} %fields_hbm.1, bf16[64,256]{1,0:T(8,128)(2,1)} %we_hbm.1, bf16[1,256,256]{2,1,0:T(8,128)(2,1)} %ws_hbm.1, bf16[1,256,256]{2,1,0:T(8,128)(2,1)} %wr_hbm.1, bf16[1,256,256]{2,1,0:T(8,128)(2,1)} %wu_hbm.1, bf16[1,256]{1,0:T(2,128)(2,1)} %gain_hbm.1, ...), custom_call_target="tpu_custom_call" | custom-call | tf_op jit(solution)/shard_map/cycle/pallas_call | solution.py:597
  48.8 0.8 %hand_on.1 = bf16[32,64,128]{2,1,0:T(8,128)(2,1)} custom-call(bf16[32,64,128]{2,1,0:T(8,128)(2,1)S(1)} %cycle.1.source), custom_call_target="tpu_custom_call" | custom-call | tf_op jit(solution)/shard_map/hand_on/pallas_call | solution.py:674
